TPU v7x, 32 devices: a whole 2x2x4 slice. The times are simulated.
32 devices in a mesh: shard: 2 (over x), ctx: 4 (over z), tp: 4 (over y, core).
Axes of the slice: x: 2, y: 2, z: 4, core: 2. Of those that a mesh axis runs over, the one named last changes fastest.
Arguments:
- hidden: bfloat16 [2, 4096, 1024], P('shard', ('ctx', 'tp')), may hold values from -6 to 6
- segments: int32 [2, 4096], P('shard'), may hold values from 0 to 7, never falling along the last dimension, each value on 1 to 2048 neighbouring positions
- cotangent: bfloat16 [2, 4096, 1024], P('shard', ('ctx', 'tp')), may hold values from -6 to 6
- attn_gain: bfloat16 [1024], P('shard'), may hold values from 0.25 to 1.75
- w_query: bfloat16 [1024, 2048], P('shard', 'tp'), may hold values from -0.1875 to 0.1875
- key_weight_matrix: bfloat16 [1024, 1024], P('shard', 'tp'), may hold values from -0.1875 to 0.1875
- value_weight_matrix: bfloat16 [1024, 1024], P('shard', 'tp'), may hold values from -0.1875 to 0.1875
- query_gain: bfloat16 [128], P('shard'), may hold values from 0.25 to 1.75
- key_gain: bfloat16 [128], P('shard'), may hold values from 0.25 to 1.75
- mixer_exit_coefficients: bfloat16 [2048, 1024], P('tp', 'shard'), may hold values from -0.5 to 0.5
- mlp_gain: bfloat16 [1024], P('shard'), may hold values from 0.25 to 1.75
- w_gate: bfloat16 [1024, 3072], P('shard', 'tp'), may hold values from -0.1875 to 0.1875
- w_up: bfloat16 [1024, 3072], P('shard', 'tp'), may hold values from -0.1875 to 0.1875
- w_down: bfloat16 [3072, 1024], P('tp', 'shard'), may hold values from -0.109375 to 0.109375
Outputs:
- out_hidden: bfloat16 [2, 4096, 1024], P('shard', ('ctx', 'tp'))
- grad_hidden: float32 [2, 4096, 1024], P('shard', ('ctx', 'tp'))
- grad_attn_gain: float32 [1024], P('shard')
- grad_w_query: float32 [1024, 2048], P('shard', 'tp')
- grad_w_key: float32 [1024, 1024], P('shard', 'tp')
- grad_w_value: float32 [1024, 1024], P('shard', 'tp')
- grad_query_gain: float32 [128], P('shard')
- grad_key_gain: float32 [128], P('shard')
- grad_w_output: float32 [2048, 1024], P('tp', 'shard')
- grad_mlp_gain: float32 [1024], P('shard')
- grad_w_gate: float32 [1024, 3072], P('shard', 'tp')
- grad_w_up: float32 [1024, 3072], P('shard', 'tp')
- grad_w_down: float32 [3072, 1024], P('tp', 'shard')
Inputs may be any that keep to these rules, and one draw needn't show every extreme that they name: `segments`: along each sequence the segment numbers never fall and every number from 0 to 7 occurs; a document has 1 to 2048 tokens, and one has exactly 2048.
All inputs are finite; a program needn't handle non-finite values.
Results may differ from a plain program's by a relative error of at most 0.022.
Values may be sent and summed in bfloat16 or wider, within the bound.
A program may use at most 192 MiB of HBM per device.

v0:
```python
import functools
import math

import jax
import jax.numpy as jnp
import numpy as np
from jax import lax
from jax.experimental import pallas as pl
from jax.experimental.pallas import tpu as pltpu
from jax.sharding import PartitionSpec as P

SHARD_AXIS, CTX_AXIS, TP_AXIS = "shard", "ctx", "tp"
HEAD_SIZE = 128
NDOC = 8


norm_eps = 1e-06
rope_base = 1000000.0
masked_fill = -1e30


def rms_scale(values):
    return lax.rsqrt(jnp.mean(values * values, axis=-1, keepdims=True) + norm_eps)


def rms_back(grad_out, values, row_scale, gain_vec):
    scaled = grad_out * gain_vec
    inner_sum = jnp.mean(scaled * values, axis=-1, keepdims=True)
    return row_scale * scaled - values * (row_scale * row_scale * row_scale) * inner_sum


def doc_positions(segments):
    seq_width = segments.shape[-1]
    labels = jnp.arange(NDOC, dtype=jnp.int32)
    onehot = (segments[..., None] == labels).astype(jnp.int32)
    counts = jnp.sum(onehot, axis=-2)
    starts = jnp.cumsum(counts, axis=-1) - counts
    first_row = jnp.sum(onehot * starts[..., None, :], axis=-1)
    return jnp.arange(seq_width, dtype=jnp.int32) - first_row


def rope_tables(positions):
    exponents = jnp.arange(0, HEAD_SIZE, 2).astype(jnp.float32) / HEAD_SIZE
    angle_rates = jnp.power(jnp.float32(rope_base), -exponents)
    angles = positions.astype(jnp.float32)[..., None] * angle_rates
    angles = jnp.concatenate([angles, angles], axis=-1)[..., None, :]
    return (jnp.cos(angles), jnp.sin(angles))


def rotate(inputs, cosine, sine_part):
    half_dim = inputs.shape[-1] // 2
    turned = jnp.concatenate([-inputs[..., half_dim:], inputs[..., :half_dim]], axis=-1)
    return inputs * cosine + turned * sine_part


def rotate_back(grads, cosine, sine_part):
    half_dim = grads.shape[-1] // 2
    moved = grads * sine_part
    turned = jnp.concatenate([moved[..., half_dim:], -moved[..., :half_dim]], axis=-1)
    return grads * cosine + turned


def tp_rows(local_part):
    return lax.all_gather(local_part, TP_AXIS, axis=1, tiled=True)


def tp_total(partial_sum):
    return lax.psum_scatter(
        partial_sum.astype(jnp.bfloat16), TP_AXIS, scatter_dimension=1, tiled=True
    ).astype(jnp.float32)


def key_block(segments, key_first, step_rows, query_pos, query_seg):
    key_pos = key_first + jnp.arange(step_rows, dtype=jnp.int32)
    key_seg = lax.dynamic_slice_in_dim(segments, key_first, step_rows, 1)
    allowed = (key_pos[None, None, :] <= query_pos[None, :, None]) & (
        key_seg[:, None, :] == query_seg[:, :, None]
    )
    return allowed[:, None, None]


def keep_state(state):
    return state


CHUNKS = 15
FROM_MLP = 9
READY = 2
UNITS, EARLY, MATED, LATE = 2 * CHUNKS, 2 * FROM_MLP, 2 * READY, 22


MESH_ID = pl.DeviceIdType.MESH
ANY_SPEC = pl.BlockSpec(memory_space=pl.ANY)
VMEM_SPEC = pl.BlockSpec(memory_space=pltpu.VMEM)
SCORE_STEP = HEAD_SIZE ** (-0.5) * math.log2(math.e)
APART = 16384.0


def enter(peers):
    barrier = pltpu.get_barrier_semaphore()
    for peer in peers:
        pl.semaphore_signal(barrier, inc=1, device_id=peer, device_id_type=MESH_ID)
    pl.semaphore_wait(barrier, len(peers))


def last_dot(left, right):
    return lax.dot_general(
        left, right, (((1,), (1,)), ((), ())), preferred_element_type=jnp.float32
    )


def flat_dot(left, right):
    return jnp.dot(left, right, preferred_element_type=jnp.float32)


def first_dot(left, right):
    return lax.dot_general(
        left, right, (((0,), (0,)), ((), ())), preferred_element_type=jnp.float32
    )


def spin(values, cosine, sine_signed):
    return values * cosine + pltpu.roll(values, HEAD_SIZE // 2, 1) * sine_signed


class Links:
    def __init__(self, send, recv):
        self.send, self.recv, self.used = send, recv, 0

    def copy(self, src, dst, device):
        number = self.used
        self.used += 1
        return pltpu.make_async_remote_copy(
            src_ref=src, dst_ref=dst, send_sem=self.send.at[number],
            recv_sem=self.recv.at[number], device_id=device, device_id_type=MESH_ID,
        )


class Locals:
    def __init__(self, sems):
        self.sems, self.used, self.open = sems, 0, []

    def make(self, src, dst):
        copy = pltpu.make_async_copy(src, dst, self.sems.at[self.used])
        self.used += 1
        return copy

    def start(self, src, dst):
        copy = self.make(src, dst)
        copy.start()
        self.open.append(copy)
        return copy

    def wait(self, copy):
        copy.wait()
        self.open = [other for other in self.open if other is not copy]

    def finish(self):
        for copy in self.open:
            copy.wait()


def forward_kernel(
    hidden, cotangent, gains_own, segments, rates, wq, wk, wv, wo, wg, wu,
    gains_out, rows_out, q_out, k_out, query_out, keys_out, values_out, cos_out, sin_out,
    attended_out, low_out, wqkv_out, crows_out, wo_out, wg_out, wu_out,
    gains, raw, rows, wqkv, q_proj, k_proj, qaug, kaug, vaug, cosine, sine, acc, low, crows,
    gains_in, gains_land, places, send, recv, local,
):
    s, c, t = lax.axis_index(SHARD_AXIS), lax.axis_index(CTX_AXIS), lax.axis_index(TP_AXIS)
    nctx = lax.axis_size(CTX_AXIS)
    part = hidden.shape[0]
    block = 4 * part
    half = wq.shape[0]
    f32, bf16 = jnp.float32, jnp.bfloat16
    side, across, mate = {TP_AXIS: t ^ 1}, {TP_AXIS: t ^ 2}, {SHARD_AXIS: 1 - s}
    pair = {CTX_AXIS: c ^ 1}
    nxt, prv = {CTX_AXIS: lax.rem(c + 1, nctx)}, {CTX_AXIS: lax.rem(c + nctx - 1, nctx)}
    gains_in[...] = jnp.zeros(gains_in.shape, f32)
    for row in range(2):
        own_gain = gains_own[:, row * half : row * half + half].astype(f32)
        gains_in[row : row + 1, pl.ds(pl.multiple_of(s * half, half), half)] = own_gain
    small = jnp.broadcast_to(gains_own[:, 2 * half : 2 * half + HEAD_SIZE], (16, HEAD_SIZE))
    square = (HEAD_SIZE, HEAD_SIZE)
    source_lane = lax.broadcasted_iota(jnp.int32, square, 0)
    target_lane = lax.broadcasted_iota(jnp.int32, square, 1) - s * (HEAD_SIZE // 2)
    for row, first in ((2, 0), (3, HEAD_SIZE // 2)):
        chosen = (source_lane - first == target_lane) & (source_lane >= first)
        chosen = chosen & (source_lane < first + HEAD_SIZE // 2)
        placed = flat_dot(small, jnp.where(chosen, 1.0, 0.0).astype(bf16))
        gains_in[row : row + 1, 0:HEAD_SIZE] = placed[0:1]
    enter([side, across, mate, nxt, prv])
    links, locals_ = Links(send, recv), Locals(local)

    def piece(owner):
        return pl.ds(pl.multiple_of(owner * part, part), part)

    low_bit = c & 1

    def some(shard, count, size):
        return pl.ds(pl.multiple_of(shard * count + low_bit * size, size), size)

    mine = pl.ds(pl.multiple_of(s * half, half), half)
    quarter = half // 2
    gains_copy = links.copy(gains_in, gains_land, mate)
    wk_copy = links.copy(wk, wqkv.at[mine, 512:768], mate)
    wv_copy = links.copy(wv, wqkv.at[mine, 768:1024], mate)
    wq_copy = links.copy(wq, wqkv.at[mine, 0:512], mate)
    wo_copy = links.copy(
        wo.at[some(0, 0, quarter), :], wo_out.at[some(0, 0, quarter), :], mate
    )
    wo_got = wo_out.at[some(0, 0, quarter), :]
    wo_on = links.copy(wo_got, wo_got, pair)
    wg_copy = links.copy(
        wg.at[some(0, 0, quarter), :], wg_out.at[some(0, 0, quarter), :], mate
    )
    wg_got = wg_out.at[some(0, 0, quarter), :]
    wg_on = links.copy(wg_got, wg_got, pair)
    wu_copy = links.copy(
        wu.at[some(0, 0, quarter), :], wu_out.at[some(0, 0, quarter), :], mate
    )
    gains_copy.start()
    wk_copy.start()
    wv_copy.start()
    wq_copy.start()
    own_k = locals_.start(wk, wqkv.at[mine, 512:768])
    own_v = locals_.start(wv, wqkv.at[mine, 768:1024])
    own_q = locals_.start(wq, wqkv.at[mine, 0:512])
    own_c = locals_.start(cotangent, crows.at[piece(t), :])

    def source(b, owner):
        return hidden if b == 0 else raw.at[b, piece(owner)]

    to_across, to_side, on_to_side, to_next = [], [], [], []
    for b in range(3):
        there = raw.at[b, piece(t ^ 2)]
        to_side.append(links.copy(source(b, t), raw.at[b, piece(t)], side))
        on_to_side.append(links.copy(there, there, side))
        if b < 2:
            to_across.append(links.copy(source(b, t), raw.at[b, piece(t)], across))
            to_next.append(links.copy(source(b, t), raw.at[b + 1, piece(t)], nxt))
    far_to_next = links.copy(raw.at[1, piece(t ^ 2)], raw.at[2, piece(t ^ 2)], nxt)
    c_side = links.copy(cotangent, crows.at[piece(t), :], side)
    c_over = links.copy(cotangent, crows.at[piece(t), :], across)
    c_on = links.copy(crows.at[piece(t ^ 2), :], crows.at[piece(t ^ 2), :], side)
    to_across[0].start()
    to_side[0].start()

    @pl.when(c < nctx - 1)
    def _():
        to_next[0].start()

    c_side.start()
    raw[0, piece(t), :] = hidden[...]
    gains_copy.wait()
    gains[...] = gains_in[...] + gains_land[...]
    q_gain = gains[2:3, 0:HEAD_SIZE]
    k_gain = gains[3:4, 0:HEAD_SIZE]

    def table(b):
        start, stop, rate = places[0:1, :], places[1:2, :], rates[...]
        shape = (128, HEAD_SIZE)
        lower = lax.broadcasted_iota(jnp.int32, shape, 1) < HEAD_SIZE // 2

        @pl.loop(0, 4)
        def _(n):
            found = []
            for offset in (0, 512):
                first = n * 128 + offset
                index = (lax.broadcasted_iota(jnp.int32, shape, 0) + first) + (c - b) * block
                index = index.astype(f32)
                inside = (index >= start) & (index < stop)
                marks = jnp.where(inside, 1.0, 0.0)
                begin = jnp.sum(jnp.where(inside, start, 0.0), axis=1, keepdims=True)
                at = pl.ds(pl.multiple_of(first, 128), 128)
                for g in range(2):
                    kaug[b, g, at, 128:256] = (1.0 - marks).astype(bf16)
                if b == 0:
                    for h in range(4):
                        qaug[h, at, 128:256] = (marks * -APART).astype(bf16)
                found.append((at, index - begin))
            (low_at, low_pos), (high_at, high_pos) = found
            angle = jnp.where(lower, low_pos, high_pos) * rate
            cs, sn = jnp.cos(angle), jnp.sin(angle)
            cr, sr = pltpu.roll(cs, HEAD_SIZE // 2, 1), pltpu.roll(sn, HEAD_SIZE // 2, 1)
            cosine[b, low_at, :] = jnp.where(lower, cs, cr)
            cosine[b, high_at, :] = jnp.where(lower, cr, cs)
            sine[b, low_at, :] = jnp.where(lower, -sn, sr)
            sine[b, high_at, :] = jnp.where(lower, -sr, sn)

    def project_kv(b, owner):
        at = piece(owner)
        x = raw[b, at, :].astype(f32)
        scale = lax.rsqrt(jnp.mean(x * x, axis=-1, keepdims=True) + norm_eps)
        rows[b, at, :] = (x * scale * gains[0:1, :]).astype(bf16)
        got = flat_dot(rows[b, at, :], wqkv[:, 512:1024])
        k_proj[b, at, :] = got[:, 0:256]
        for g in range(2):
            u = got[:, g * 128 : g * 128 + 128]
            r = lax.rsqrt(jnp.mean(u * u, axis=-1, keepdims=True) + norm_eps)
            turned = spin(u * r * k_gain, cosine[b, at, :], sine[b, at, :])
            kaug[b, g, at, 0:128] = turned.astype(bf16)
            vaug[b, g, at, 0:128] = got[:, 256 + g * 128 : 384 + g * 128].astype(bf16)

    def project_q(owner):
        at = piece(owner)
        got = flat_dot(rows[0, at, :], wqkv[:, 0:512])
        q_proj[at, :] = got
        for h in range(4):
            u = got[:, h * 128 : h * 128 + 128]
            r = lax.rsqrt(jnp.mean(u * u, axis=-1, keepdims=True) + norm_eps)
            turned = spin(u * r * q_gain, cosine[0, at, :], sine[0, at, :])
            qaug[h, at, 0:128] = turned.astype(bf16)

    def unit(b, g, r, kc, bound):
        at = pl.ds(pl.multiple_of(r * 512, 512), 512)
        for hh in range(2):
            qq = qaug[2 * g + hh, at, :]
            total = None
            for j in range(2):
                keys_at = pl.ds(pl.multiple_of(kc * 512 + j * 256, 256), 256)
                p = jnp.exp2(last_dot(qq, kaug[b, g, keys_at, :]) * SCORE_STEP)
                if bound is not None:
                    ahead = lax.broadcasted_iota(jnp.int32, p.shape, 0) - lax.broadcasted_iota(
                        jnp.int32, p.shape, 1
                    )
                    p = jnp.where(ahead >= bound + j * 256, p, 0.0)
                value = flat_dot(p.astype(bf16), vaug[b, g, keys_at, :])
                total = value if total is None else total + value
            acc[2 * g + hh, at, :] += total

    def block_outs(b):
        pairs = (
            (rows, rows_out), (k_proj, k_out), (kaug, keys_out), (vaug, values_out),
            (cosine, cos_out), (sine, sin_out),
        )
        return [locals_.make(a.at[b], d.at[b]) for a, d in pairs]

    outs = [block_outs(b) for b in range(3)]

    lane = lax.broadcasted_iota(jnp.int32, (1, HEAD_SIZE), 1)
    begin = jnp.full((1, HEAD_SIZE), float(nctx * block), f32)
    end = begin
    for label in range(NDOC):
        before = jnp.where(segments[...] < label, 1.0, 0.0)
        before = jnp.sum(before, axis=(0, 1), keepdims=True)
        begin = jnp.where(lane == label, before, begin)
        end = jnp.where(lane == label - 1, before, end)
    places[0:1, :] = begin
    places[1:2, :] = end
    table(0)
    vaug[:, :, :, 128:256] = jnp.ones((3, 2, block, 128), bf16)
    acc[...] = jnp.zeros(acc.shape, f32)
    locals_.wait(own_k)
    locals_.wait(own_v)
    wk_copy.wait()
    wv_copy.wait()
    wo_copy.start()
    to_across[0].wait_recv()
    on_to_side[0].start()

    @pl.when(c >= 1)
    def _():
        to_next[0].wait_recv()
        to_across[1].start()
        to_side[1].start()

        @pl.when(c < nctx - 1)
        def _():
            to_next[1].start()

    to_side[0].wait_recv()
    on_to_side[0].wait_recv()

    @pl.loop(0, 4)
    def _(n):
        project_kv(0, n)

    for copy in outs[0]:
        copy.start()

    @pl.when(c >= 1)
    def _():
        table(1)
        to_side[1].wait_recv()

        @pl.loop(0, 2)
        def _(n):
            project_kv(1, t ^ n)

    @pl.when(c >= 2)
    def _():
        table(2)

    locals_.wait(own_q)
    wq_copy.wait()
    wg_copy.start()

    @pl.when(c >= 1)
    def _():
        to_across[1].wait_recv()
        on_to_side[1].start()

        @pl.when(c < nctx - 1)
        def _():
            far_to_next.start()

        @pl.when(c >= 2)
        def _():
            to_next[1].wait_recv()
            to_side[2].start()

    c_over.start()

    @pl.loop(0, 4)
    def _(n):
        project_q(n)

    locals_.start(q_proj, q_out)
    locals_.start(wqkv, wqkv_out)

    @pl.loop(0, 6)
    def _(n):
        m = lax.rem(n, 3)
        unit(0, n // 3, (m + 1) // 2, m // 2, (m & 1) * -512)

    wo_copy.wait_recv()
    wo_on.start()
    wu_copy.start()

    @pl.when(c >= 1)
    def _():
        on_to_side[1].wait_recv()

        @pl.loop(2, 4)
        def _(n):
            project_kv(1, t ^ n)

        for copy in outs[1]:
            copy.start()

        @pl.loop(0, 8)
        def _(n):
            m = lax.rem(n, 4)
            unit(1, n // 4, m // 2, m & 1, None)

    wg_copy.wait_recv()
    wg_on.start()

    c_over.wait_recv()
    c_on.start()

    @pl.when(c >= 2)
    def _():
        far_to_next.wait_recv()
        on_to_side[2].start()
        to_side[2].wait_recv()
        on_to_side[2].wait_recv()

        @pl.loop(0, 4)
        def _(n):
            project_kv(2, n)

        for copy in outs[2]:
            copy.start()

        @pl.loop(0, 6)
        def _(n):
            m = lax.rem(n, 3)
            unit(2, n // 3, m // 2, (m + 1) // 2, None)

    for h in range(4):

        @pl.loop(0, 4)
        def _(r):
            at = pl.ds(pl.multiple_of(r * 256, 256), 256)
            total = acc[h, at, 128:256]
            value = acc[h, at, 0:128] / total
            acc[h, at, 0:128] = value
            shift = jnp.log(total) * -(HEAD_SIZE**0.5)
            top = shift.astype(bf16).astype(f32)
            mid = (shift - top).astype(bf16).astype(f32)
            lane = lax.broadcasted_iota(jnp.int32, shift.shape, 1)
            parts = jnp.where(lane == NDOC, top, 0.0)
            parts = jnp.where(lane == NDOC + 1, mid, parts)
            parts = jnp.where(lane == NDOC + 2, shift - top - mid, parts)
            qaug[h, at, 128:256] = qaug[h, at, 128:256] + parts.astype(bf16)
            low[h, at, :] = value.astype(bf16)

        lanes = slice(h * 128, h * 128 + 128)
        locals_.start(low.at[h], low_out.at[:, lanes])
        locals_.start(acc.at[h, :, 0:128], attended_out.at[:, lanes])
        locals_.start(qaug.at[h], query_out.at[h])

    locals_.start(gains, gains_out)
    locals_.wait(own_c)
    c_side.wait()
    c_on.wait()
    locals_.start(crows, crows_out)
    c_over.wait_send()
    to_across[0].wait_send()
    to_side[0].wait_send()
    on_to_side[0].wait_send()
    for copy in outs[0]:
        copy.wait()

    @pl.when(c < nctx - 1)
    def _():
        to_next[0].wait_send()

    for b in (1, 2):

        @pl.when(c >= b)
        def _():
            if b < 2:
                to_across[b].wait_send()
            to_side[b].wait_send()
            on_to_side[b].wait_send()
            for copy in outs[b]:
                copy.wait()

    @pl.when((c >= 1) & (c < nctx - 1))
    def _():
        to_next[1].wait_send()
        far_to_next.wait_send()

    wo_copy.wait_send()
    wo_on.wait()
    wg_copy.wait_send()
    wg_on.wait()
    wu_copy.wait()
    locals_.finish()


def forward_call(hidden, cotangent, gains, segments, rates, wq, wk, wv, wo, wg, wu):
    part, width = hidden.shape
    block = 4 * part
    f32, bf16 = jnp.float32, jnp.bfloat16
    shape = jax.ShapeDtypeStruct
    outs = (
        shape((8, width), f32),
        shape((3, block, width), bf16),
        shape((block, 512), f32),
        shape((3, block, 256), f32),
        shape((4, block, 256), bf16),
        shape((3, 2, block, 256), bf16),
        shape((3, 2, block, 256), bf16),
        shape((3, block, HEAD_SIZE), f32),
        shape((3, block, HEAD_SIZE), f32),
        shape((block, 512), f32),
        shape((block, 512), bf16),
        shape((width, 1024), bf16),
        shape((block, width), bf16),
        shape(wo.shape, bf16),
        shape(wg.shape, bf16),
        shape(wu.shape, bf16),
    )
    return pl.pallas_call(
        forward_kernel,
        name="forward",
        out_shape=outs,
        in_specs=[VMEM_SPEC] * 5 + [ANY_SPEC] * 6,
        out_specs=[ANY_SPEC] * len(outs),
        scratch_shapes=[
            pltpu.VMEM((8, width), f32),
            pltpu.VMEM((3, block, width), bf16),
            pltpu.VMEM((3, block, width), bf16),
            pltpu.VMEM((width, 1024), bf16),
            pltpu.VMEM((block, 512), f32),
            pltpu.VMEM((3, block, 256), f32),
            pltpu.VMEM((4, block, 256), bf16),
            pltpu.VMEM((3, 2, block, 256), bf16),
            pltpu.VMEM((3, 2, block, 256), bf16),
            pltpu.VMEM((3, block, HEAD_SIZE), f32),
            pltpu.VMEM((3, block, HEAD_SIZE), f32),
            pltpu.VMEM((4, block, 256), f32),
            pltpu.VMEM((4, block, 128), bf16),
            pltpu.VMEM((block, width), bf16),
            pltpu.VMEM((8, width), f32),
            pltpu.VMEM((8, width), f32),
            pltpu.VMEM((8, HEAD_SIZE), f32),
            pltpu.SemaphoreType.DMA((23,)),
            pltpu.SemaphoreType.DMA((23,)),
            pltpu.SemaphoreType.DMA((38,)),
        ],
        compiler_params=pltpu.CompilerParams(
            collective_id=0, has_side_effects=True, vmem_limit_bytes=58 << 20
        ),
    )(hidden, cotangent, gains, segments, rates, wq, wk, wv, wo, wg, wu)


class Scatter:
    def __init__(self, links, bufs, side, across):
        self.bufs = bufs
        self.far = links.copy(bufs.at[0], bufs.at[3], side)
        self.over = links.copy(bufs.at[1], bufs.at[4], across)
        self.near = links.copy(bufs.at[2], bufs.at[5], side)

    def put_far(self, value):
        self.bufs[0] = value.astype(jnp.bfloat16)
        self.far.start()

    def put_over(self, value):
        self.far.wait_recv()
        self.bufs[1] = (value + self.bufs[3].astype(jnp.float32)).astype(jnp.bfloat16)
        self.over.start()

    def put_near(self, value):
        self.bufs[2] = value.astype(jnp.bfloat16)
        self.near.start()

    def total(self, value):
        self.near.wait_recv()
        self.over.wait_recv()
        return value + self.bufs[5].astype(jnp.float32) + self.bufs[4].astype(jnp.float32)

    def close(self):
        self.far.wait_send()
        self.over.wait_send()
        self.near.wait_send()


def mlp_kernel(
    low, hidden, gains, crows_in, wo_own, wo_got, wg_own, wg_got, wu_own, wu_got,
    wd,
    d_middle_out, gain_out, brow_out, own_out, give_out, parts_out, out_own_out,
    wo, wgf, wuf, wdf, mrows, act, dgate, dup, brow, kept, middle, bufs, parts, give, own, land,
    crows, result, send, recv, local,
):
    s, c, t = lax.axis_index(SHARD_AXIS), lax.axis_index(CTX_AXIS), lax.axis_index(TP_AXIS)
    part = hidden.shape[0]
    half = wd.shape[1]
    bf16, f32 = jnp.bfloat16, jnp.float32
    side, across = {TP_AXIS: t ^ 1}, {TP_AXIS: t ^ 2}
    mate, pair = {SHARD_AXIS: 1 - s}, {CTX_AXIS: c ^ 1}
    links, locals_ = Links(send, recv), Locals(local)

    def piece(owner):
        return pl.ds(pl.multiple_of(owner * part, part), part)

    mine = pl.ds(pl.multiple_of(s * half, half), half)
    theirs = pl.ds(pl.multiple_of((1 - s) * half, half), half)
    low_bit = c & 1

    def some(shard, count, size):
        return pl.ds(pl.multiple_of(shard * count + low_bit * size, size), size)

    quarter = half // 2
    third = wd.shape[0] // 2
    wu_at = some(1 - s, half, quarter)
    wu_on = links.copy(wu_got.at[some(0, 0, quarter), :], wuf.at[wu_at, :], pair)
    wd_copy = links.copy(
        wd.at[some(0, 0, third), :], wdf.at[some(0, 0, third), mine], mate
    )
    wd_got = wdf.at[some(0, 0, third), theirs]
    wd_on = links.copy(wd_got, wd_got, pair)
    wo_loads = [
        locals_.start(wo_own, wo.at[:, mine]),
        locals_.start(wo_got, wo.at[:, theirs]),
    ]
    enter([side, across, mate, pair])
    wu_on.start()
    wd_copy.start()
    own_weights = [
        locals_.start(wg_own, wgf.at[mine, :]),
        locals_.start(wg_got, wgf.at[theirs, :]),
        locals_.start(wu_own, wuf.at[mine, :]),
        locals_.start(wu_got.at[some(0, 0, quarter), :], wuf.at[wu_at, :]),
        locals_.start(wd, wdf.at[:, mine]),
        locals_.start(crows_in, crows),
    ]
    for copy in wo_loads:
        locals_.wait(copy)

    branch = Scatter(links, bufs.at[0], side, across)
    back = Scatter(links, bufs.at[1], side, across)

    def branch_part(owner):
        return flat_dot(low[piece(owner), :], wo[...])

    @pl.loop(0, 4)
    def _(n):
        value = branch_part(t ^ (3 - n))
        pl.when(n == 0)(lambda: branch.put_far(value))
        pl.when(n == 1)(lambda: branch.put_over(value))
        pl.when(n == 2)(lambda: branch.put_near(value))

        @pl.when(n == 3)
        def _():
            middle[...] = hidden[...].astype(f32) + value

    wd_copy.wait_recv()
    wd_on.start()
    middle[...] = branch.total(middle[...])
    m = middle[...]
    scale = lax.rsqrt(jnp.mean(m * m, axis=-1, keepdims=True) + norm_eps)
    gain = gains[1:2, :]
    mrows[piece(t), :] = (m * scale * gain).astype(bf16)
    here, there = mrows.at[piece(t), :], mrows.at[piece(t ^ 2), :]
    m_over, m_near = links.copy(here, here, across), links.copy(here, here, side)
    m_on = links.copy(there, there, side)
    m_over.start()
    m_near.start()
    for copy in own_weights:
        locals_.wait(copy)
    wu_on.wait_recv()
    wd_on.wait_recv()

    def mlp(owner):
        at = piece(owner)
        rows = mrows[at, :]
        gate = flat_dot(rows, wgf[...])
        upward = flat_dot(rows, wuf[...])
        d_act = last_dot(crows[at, :], wdf[...])
        sig = 1.0 / (1.0 + jnp.exp(-gate))
        silu = gate * sig
        act[at, :] = (silu * upward).astype(bf16)
        dup[at, :] = (d_act * silu).astype(bf16)
        dgate[at, :] = (d_act * upward * sig * (1.0 + gate * (1.0 - sig))).astype(bf16)

    def out_part(owner):
        return flat_dot(act[piece(owner), :], wdf[...])

    def back_part(owner):
        at = piece(owner)
        return last_dot(dgate[at, :], wgf[...]) + last_dot(dup[at, :], wuf[...])

    m_near.wait_recv()

    @pl.loop(0, 4)
    def _(n):
        @pl.when(n == 2)
        def _():
            m_over.wait_recv()
            m_on.start()
            m_on.wait_recv()

        owner = t ^ jnp.where(n < 2, n, 5 - n)
        mlp(owner)
        value = back_part(owner)

        @pl.when(n == 0)
        def _():
            kept[0] = value

        pl.when(n == 1)(lambda: back.put_near(value))
        pl.when(n == 2)(lambda: back.put_far(value))
        pl.when(n == 3)(lambda: back.put_over(value))

    to_mate = [links.copy(give.at[k], land.at[k], mate) for k in range(READY)]

    def lanes(n):
        return pl.ds(pl.multiple_of(n * 256, 256), 256)

    def down_chunk(ref, n, columns):
        ref[n] = first_dot(act[:, lanes(n)], crows[:, columns]).astype(bf16)

    def wide_chunk(ref, k, grads, n, columns):
        got = first_dot(mrows[:, columns], grads[:, lanes(n)]).astype(bf16)
        ref[k + n, :, 0:256] = got[0:256]
        ref[k + n, :, 256:512] = got[256:512]

    @pl.loop(0, 3)
    def _(n):
        down_chunk(give, n, theirs)

    for copy in to_mate:
        copy.start()

    @pl.loop(0, 3)
    def _(n):
        down_chunk(own, n, mine)
        for k, grads in ((3, dgate), (6, dup)):
            wide_chunk(give, k, grads, n, theirs)
            wide_chunk(own, k, grads, n, mine)

    @pl.loop(0, 4)
    def _(n):
        value = out_part(t ^ (3 - n))

        @pl.when(n < 3)
        def _():
            parts[n] = value.astype(bf16)

        @pl.when(n == 3)
        def _():
            kept[1] = value + middle[...]

    locals_.start(kept.at[1], out_own_out)
    locals_.start(parts, parts_out)
    locals_.start(give.at[READY:FROM_MLP], give_out)
    locals_.start(own.at[READY:FROM_MLP], own_out.at[READY:FROM_MLP])

    d_mlp = back.total(kept[0])
    m = middle[...]
    scale = lax.rsqrt(jnp.mean(m * m, axis=-1, keepdims=True) + norm_eps)
    scaled = d_mlp * gain
    inner = jnp.mean(scaled * m, axis=-1, keepdims=True)
    d_middle = (
        crows[piece(t), :].astype(f32) + scale * scaled - m * (scale * scale * scale) * inner
    )
    kept[0] = d_middle
    gain_grad = jnp.sum(d_mlp * m * scale, axis=0, keepdims=True)
    brow[...] = d_middle.astype(bf16)
    locals_.start(brow, brow_out)
    locals_.start(kept.at[0], d_middle_out)
    result[...] = jnp.broadcast_to(gain_grad, (8, gain_grad.shape[1]))
    locals_.start(result, gain_out)

    for k in range(READY):
        to_mate[k].wait_recv()
        own[k] = own[k] + land[k]
    locals_.start(own.at[0:READY], own_out.at[0:READY])
    for k in range(READY):
        to_mate[k].wait_send()
    wu_on.wait_send()
    wd_copy.wait_send()
    wd_on.wait_send()
    branch.close()
    back.close()
    for copy in (m_over, m_near, m_on):
        copy.wait_send()
    locals_.finish()


def mlp_call(vmem_args, any_args):
    low, hidden, gains = vmem_args
    wo, wd = any_args[1], any_args[-1]
    part, width = hidden.shape
    block = 4 * part
    units = wd.shape[0]
    f32, bf16 = jnp.float32, jnp.bfloat16
    shape = jax.ShapeDtypeStruct
    outs = (
        shape((part, width), f32),
        shape((8, width), f32),
        shape((part, width), bf16),
        shape((FROM_MLP, 256, 512), bf16),
        shape((FROM_MLP - READY, 256, 512), bf16),
        shape((3, part, width), bf16),
        shape((part, width), f32),
    )
    return pl.pallas_call(
        mlp_kernel,
        name="mlp",
        out_shape=outs,
        in_specs=[VMEM_SPEC] * 3 + [ANY_SPEC] * 8,
        out_specs=[ANY_SPEC] * len(outs),
        scratch_shapes=[
            pltpu.VMEM((wo.shape[0], width), bf16),
            pltpu.VMEM((width, units), bf16),
            pltpu.VMEM((width, units), bf16),
            pltpu.VMEM((units, width), bf16),
            pltpu.VMEM((block, width), bf16),
            pltpu.VMEM((block, units), bf16),
            pltpu.VMEM((block, units), bf16),
            pltpu.VMEM((block, units), bf16),
            pltpu.VMEM((part, width), bf16),
            pltpu.VMEM((2, part, width), f32),
            pltpu.VMEM((part, width), f32),
            pltpu.VMEM((2, 6, part, width), bf16),
            pltpu.VMEM((3, part, width), bf16),
            pltpu.VMEM((FROM_MLP, 256, 512), bf16),
            pltpu.VMEM((FROM_MLP, 256, 512), bf16),
            pltpu.VMEM((READY, 256, 512), bf16),
            pltpu.VMEM((block, width), bf16),
            pltpu.VMEM((8, width), f32),
            pltpu.SemaphoreType.DMA((12 + READY,)),
            pltpu.SemaphoreType.DMA((12 + READY,)),
            pltpu.SemaphoreType.DMA((16,)),
        ],
        compiler_params=pltpu.CompilerParams(
            collective_id=1, has_side_effects=True, vmem_limit_bytes=58 << 20
        ),
    )(*vmem_args, *any_args)


class Pump:
    def __init__(self, refs, sems, mate, near, opposite, outer, out, first_mate):
        self.own, self.mated, self.landed, self.summed = refs
        self.send, self.recv, self.local = sems
        self.mate, self.near, self.opposite, self.outer = mate, near, opposite, outer
        self.inner = jnp.logical_not(outer)
        self.out, self.first_mate = out, first_mate

    def remote(self, stage, u, src, dst, device):
        return pltpu.make_async_remote_copy(
            src_ref=src, dst_ref=dst, send_sem=self.send.at[stage * UNITS + u],
            recv_sem=self.recv.at[stage * UNITS + u], device_id=device, device_id_type=MESH_ID,
        )

    def to_mate(self, u, src):
        return self.remote(0, u, src, self.mated.at[u - self.first_mate], self.mate)

    def inward(self, u):
        return self.remote(1, u, self.own.at[u], self.landed.at[u], self.near)

    def cross(self, u):
        return self.remote(2, u, self.landed.at[u], self.summed.at[u], self.opposite)

    def outward(self, u):
        return self.remote(3, u, self.summed.at[u], self.landed.at[u], self.near)

    def write(self, u, ref):
        return pltpu.make_async_copy(ref.at[u], self.out.at[u], self.local.at[u])

    def run(self, condition, body):
        if isinstance(condition, bool):
            if condition:
                body()
        else:
            pl.when(condition)(body)

    def first(self, u):
        def bring():
            self.to_mate(u, self.own.at[u]).wait_recv()
            self.own[u] = self.own[u] + self.mated[u - self.first_mate]

        self.run(u >= self.first_mate, bring)
        pl.when(self.outer)(lambda: self.inward(u).start())

    def second(self, u):
        @pl.when(self.inner)
        def _():
            self.inward(u).wait_recv()
            self.landed[u] = self.own[u] + self.landed[u]
            self.cross(u).start()

    def third(self, u):
        @pl.when(self.inner)
        def _():
            self.cross(u).wait_recv()
            self.summed[u] = self.landed[u] + self.summed[u]
            self.outward(u).start()
            self.write(u, self.summed).start()

    def fourth(self, u):
        @pl.when(self.outer)
        def _():
            self.outward(u).wait_recv()
            self.write(u, self.landed).start()

    def slot(self, k):
        for u in (2 * k, 2 * k + 1):
            self.first(u)
            self.run(k >= 2, lambda: self.second(u - 4))
            self.run(k >= 4, lambda: self.third(u - 8))

    def close(self):
        @pl.loop(0, UNITS)
        def _(u):
            pl.when(self.outer)(lambda: self.inward(u).wait_send())

            @pl.when(self.inner)
            def _():
                self.cross(u).wait_send()
                self.outward(u).wait_send()

            self.write(u, self.summed).wait()


def backward_kernel(
    query, gains, mlp_gain_grad, hidden, brow_in, low, attended, wo_own, wo_got, d_middle,
    q_proj_in, wqkv_in, own_in, give, parts, out_own, keys, values, k_proj, cosine, sine, rows,
    hidden_out, hidden_grad, gains_out, sums_out,
    kbuf, vbuf, kpbuf, cosbuf, sinbuf, rowbuf, dq, dk, dv, dkv, dqp, gkv, kept, bufs,
    own, mated, landed, summed, late_give, far_land, mid_land, out_buf,
    dout, q_proj, wqkv,
    gsum, gland, send, recv, pump_send, pump_recv, pump_local, local, blocksem,
):
    s, c, t = lax.axis_index(SHARD_AXIS), lax.axis_index(CTX_AXIS), lax.axis_index(TP_AXIS)
    nctx = lax.axis_size(CTX_AXIS)
    part = hidden.shape[0]
    half = rows.shape[2] // 2
    f32, bf16 = jnp.float32, jnp.bfloat16
    side, across, mate = {TP_AXIS: t ^ 1}, {TP_AXIS: t ^ 2}, {SHARD_AXIS: 1 - s}
    near, opposite = {CTX_AXIS: c ^ 1}, {CTX_AXIS: c ^ 3}
    previous = {CTX_AXIS: lax.rem(c + nctx - 1, nctx)}
    outer = (c == 0) | (c == nctx - 1)
    links, locals_ = Links(send, recv), Locals(local)
    scale = HEAD_SIZE ** (-0.5)
    pump = Pump(
        (own, mated, landed, summed), (pump_send, pump_recv, pump_local),
        mate, near, opposite, outer, sums_out, MATED,
    )

    def piece(owner):
        return pl.ds(pl.multiple_of(owner * part, part), part)

    mine = pl.ds(pl.multiple_of(s * half, half), half)
    theirs = pl.ds(pl.multiple_of((1 - s) * half, half), half)

    def half_at(ref_shard, n, size):
        return pl.ds(pl.multiple_of(ref_shard * half + n * size, size), size)

    def block_copies(b):
        slot = b & 1
        pairs = (
            (keys.at[b], kbuf.at[slot]), (values.at[b], vbuf.at[slot]),
        )
        return [
            pltpu.make_async_copy(a, d, blocksem.at[6 * b + n]) for n, (a, d) in enumerate(pairs)
        ]

    def row_copies(b):
        pairs = (
            (k_proj.at[b], kpbuf), (cosine.at[b], cosbuf), (sine.at[b], sinbuf),
            (rows.at[b], rowbuf),
        )
        return [
            pltpu.make_async_copy(a, d, blocksem.at[6 * b + 2 + n])
            for n, (a, d) in enumerate(pairs)
        ]

    def row_fetch(b):
        for copy in row_copies(b):
            copy.start()

    def fetch(b):
        for copy in block_copies(b):
            copy.start()

    def fetched(b):
        for copy in block_copies(b):
            copy.wait()

    brow_load = locals_.start(brow_in, rowbuf.at[piece(t), :])
    loads = [locals_.start(own_in, own.at[0:EARLY])]
    wo_loads = []
    for j in range(2):
        at = slice(j * 256, j * 256 + 256)
        wo_loads.append(locals_.start(wo_own.at[at, :], bufs.at[1, j, :, mine]))
        wo_loads.append(locals_.start(wo_got.at[at, :], bufs.at[1, j, :, theirs]))
    for h in range(4):
        wo_loads.append(locals_.start(attended.at[:, h * 128 : h * 128 + 128], dq.at[h]))
    wo_loads.append(locals_.start(low, dkv))
    out_loads = [locals_.start(parts.at[1], out_buf.at[0]), locals_.start(out_own, kept.at[1])]

    @pl.when(c >= 2)
    def _():
        fetch(2)

    @pl.when(c >= 1)
    def _():
        fetch(1)

    @pl.when(c <= 1)
    def _():
        fetch(0)

    late_loads = [locals_.start(q_proj_in, q_proj), locals_.start(wqkv_in, wqkv)]
    enter([side, across, mate, near, opposite])

    def send_early(first, count):
        for u in range(first, min(first + count, EARLY)):
            pump.to_mate(u, give.at[u - MATED]).start()

    here, there = rowbuf.at[piece(t), :], rowbuf.at[piece(t ^ 2), :]
    b_over, b_near = links.copy(here, here, across), links.copy(here, here, side)
    b_on = links.copy(there, there, side)
    locals_.wait(brow_load)
    b_over.start()
    b_near.start()
    send_early(MATED, 4)
    out_far = links.copy(parts.at[0], out_buf.at[1], side)
    out_over = links.copy(out_buf.at[0], out_buf.at[2], across)
    out_near = links.copy(parts.at[2], out_buf.at[3], side)
    out_far.start()
    out_near.start()
    scatters = [
        Scatter(links, bufs.at[0], side, across),
        Scatter(links, bufs.at[1], side, across),
        Scatter(links, bufs.at[0], side, across),
    ]
    far_copy = links.copy(out_buf.at[0], far_land, previous)
    mid_copy = links.copy(out_buf.at[1], mid_land, previous)
    for copy in loads:
        locals_.wait(copy)
    pump.slot(0)
    send_early(MATED + 4, 2)
    gkv[...] = jnp.zeros(gkv.shape, f32)
    gsum[...] = jnp.zeros(gsum.shape, f32)
    gsum[1:2, :] = mlp_gain_grad[0:1, :]
    q_gain = gains[2:3, 0:HEAD_SIZE]
    k_gain = gains[3:4, 0:HEAD_SIZE]
    def attended_back(owner):
        at = piece(owner)
        for j in range(2):
            got = last_dot(rowbuf[at, :], bufs[1, j]).astype(bf16)
            for hh in range(2):
                h = 2 * j + hh
                head = got[:, hh * 128 : hh * 128 + 128]
                delta = -jnp.sum(head.astype(f32) * dq[h, at, :], axis=1, keepdims=True)
                top = delta.astype(bf16).astype(f32)
                lane = lax.broadcasted_iota(jnp.int32, (part, HEAD_SIZE), 1)
                extra = jnp.where(lane == 0, top, jnp.where(lane == 1, delta - top, 0.0))
                dout[h, at, 0:128] = head
                dout[h, at, 128:256] = extra.astype(bf16)

    for copy in wo_loads:
        locals_.wait(copy)
    b_near.wait_recv()

    @pl.loop(0, 2)
    def _(n):
        attended_back(t ^ n)

    for copy in out_loads:
        locals_.wait(copy)
    out_far.wait_recv()
    out_buf[0] = out_buf[0] + out_buf[1]
    pump.slot(1)
    send_early(MATED + 6, 2)
    b_over.wait_recv()
    b_on.start()
    out_over.start()
    b_on.wait_recv()

    @pl.loop(2, 4)
    def _(n):
        attended_back(t ^ n)

    for copy in (b_over, b_near, b_on):
        copy.wait_send()
    @pl.loop(0, 2)
    def _(n):
        at = pl.ds(pl.multiple_of(n * 256, 256), 256)
        for columns, target, first in ((theirs, late_give, 0), (mine, own, EARLY)):
            got = first_dot(dkv[:, at], rowbuf[:, columns]).astype(bf16)
            for e in range(2):
                target[first + 2 * n + e] = got[e * 128 : e * 128 + 128]

    for n in range(4):
        pump.to_mate(EARLY + n, late_give.at[n]).start()
    dq[...] = jnp.zeros(dq.shape, f32)
    for b in range(3):
        pl.when((c == b) if b < 2 else (c >= b))(functools.partial(row_fetch, b))
    pump.slot(2)
    send_early(MATED + 8, 2)

    def tile(b, g, r, kc, bound):
        slot = b & 1
        q_at = pl.ds(pl.multiple_of(r * 512, 512), 512)
        k_at = pl.ds(pl.multiple_of(kc * 512, 512), 512)
        kk, vv = kbuf[slot, g, k_at, :], vbuf[slot, g, k_at, :]
        dv_new, dk_new = [], []
        for hh in range(2):
            h = 2 * g + hh
            qq, do = query[h, q_at, :], dout[h, q_at, :]
            p = jnp.exp2(last_dot(qq, kk) * SCORE_STEP)
            if bound is not None:
                ahead = lax.broadcasted_iota(jnp.int32, p.shape, 0) - lax.broadcasted_iota(
                    jnp.int32, p.shape, 1
                )
                p = jnp.where(ahead >= bound, p, 0.0)
            ds = (p * last_dot(do, vv)).astype(bf16)
            dv_new.append(first_dot(do[:, 0:HEAD_SIZE], p.astype(bf16)))
            dk_new.append(first_dot(qq[:, 0:HEAD_SIZE], ds))
            dq[h, q_at, :] += flat_dot(ds, kk[:, 0:HEAD_SIZE])
        dv[g, :, k_at] += dv_new[0] + dv_new[1]
        dk[g, :, k_at] += dk_new[0] + dk_new[1]

    def clear():
        dk[...] = jnp.zeros(dk.shape, f32)
        dv[...] = jnp.zeros(dv.shape, f32)

    def norm_back(grad, u, gain, cos, sin, row):
        turned = grad * cos - pltpu.roll(grad, HEAD_SIZE // 2, 1) * sin
        r = lax.rsqrt(jnp.mean(u * u, axis=-1, keepdims=True) + norm_eps)
        gsum[row : row + 1, 0:HEAD_SIZE] += jnp.sum(turned * u * r, axis=0, keepdims=True)
        scaled = turned * gain
        inner = jnp.mean(scaled * u, axis=-1, keepdims=True)
        return (r * scaled - u * (r * r * r) * inner).astype(bf16)

    def finish_kv(b):
        for copy in row_copies(b)[:3]:
            copy.wait()

        @pl.loop(0, 4)
        def _(n):
            at = piece(n)
            cos, sin = cosbuf[at, :], sinbuf[at, :]
            for g in range(2):
                lanes = slice(g * 128, g * 128 + 128)
                u = kpbuf[at, lanes]
                dkv[at, lanes] = norm_back(dk[g, :, at].T * scale, u, k_gain, cos, sin, 3)
                dkv[at, 256 + g * 128 : 384 + g * 128] = dv[g, :, at].T.astype(bf16)

        row_copies(b)[3].wait()

        gkv[...] += first_dot(rowbuf[...], dkv[...])

    def kv_part(owner):
        return last_dot(dkv[piece(owner), :], wqkv[:, 512:1024])

    def all_part(owner):
        return kv_part(owner) + last_dot(dqp[piece(owner), :], wqkv[:, 0:512])

    def scatter(which, slot, partial):
        @pl.loop(0, 4)
        def _(n):
            value = partial(t ^ (3 - n))
            pl.when(n == 0)(lambda: which.put_far(value))
            pl.when(n == 1)(lambda: which.put_over(value))
            pl.when(n == 2)(lambda: which.put_near(value))

            @pl.when(n == 3)
            def _():
                kept[slot] = value

    for copy in late_loads:
        locals_.wait(copy)

    @pl.when(c >= 2)
    def _():
        fetched(2)
        clear()

    @pl.loop(0, 6)
    def _(n):
        m = lax.rem(n, 3)

        @pl.when(c >= 2)
        def _():
            tile(2, n // 3, m // 2, (m + 1) // 2, None)

        @pl.when(m == 2)
        def _():
            pump.slot(3 + n // 3)
            for e in range(2):
                u = MATED + 10 + 2 * (n // 3) + e
                pump.to_mate(u, give.at[u - MATED]).start()

    @pl.when(c >= 2)
    def _():
        finish_kv(2)
        fetch(0)
        row_fetch(1)
        scatter(scatters[2], 0, kv_part)

    out_near.wait_recv()
    out_over.wait_recv()
    out_buf[3] = (kept[1] + out_buf[2].astype(f32) + out_buf[3].astype(f32)).astype(bf16)
    locals_.start(out_buf.at[3], hidden_out)
    out_far.wait_send()
    out_over.wait_send()
    out_near.wait_send()
    pump.slot(5)

    @pl.when(c >= 1)
    def _():
        fetched(1)
        clear()

    @pl.loop(0, 8)
    def _(n):
        m = lax.rem(n, 4)

        @pl.when(c >= 1)
        def _():
            tile(1, n // 4, m // 2, m & 1, None)

        @pl.when(m == 3)
        def _():
            pump.slot(6 + n // 4)

    @pl.when(c >= 2)
    def _():
        out_buf[0] = scatters[2].total(kept[0]).astype(bf16)
        far_copy.start()
        scatters[2].close()

    @pl.when(c >= 1)
    def _():
        finish_kv(1)
        row_fetch(0)

    @pl.when(c >= 1)
    def _():
        scatter(scatters[1], 1, kv_part)

    pump.slot(8)
    fetched(0)
    clear()

    @pl.loop(0, 6)
    def _(n):
        m = lax.rem(n, 3)
        tile(0, n // 3, (m + 1) // 2, m // 2, (m & 1) * -512)

        @pl.when(n == 3)
        def _():
            pump.slot(9)

    finish_kv(0)

    @pl.loop(0, 4)
    def _(n):
        at = piece(n)
        cos, sin = cosbuf[at, :], sinbuf[at, :]
        for h in range(4):
            lanes = slice(h * 128, h * 128 + 128)
            u = q_proj[at, lanes]
            dqp[at, lanes] = norm_back(dq[h, at, :] * scale, u, q_gain, cos, sin, 2)

    for n in range(4):
        late_give[4 + n] = gkv[half_at(1 - s, n, 128), :].astype(bf16)
        pump.to_mate(LATE + n, late_give.at[4 + n]).start()
    for n in range(2):
        got = first_dot(rowbuf[:, half_at(1 - s, n, 256)], dqp[...]).astype(bf16)
        for e in range(2):
            late_give[8 + 2 * n + e] = got[e * 128 : e * 128 + 128]
            pump.to_mate(LATE + 4 + 2 * n + e, late_give.at[8 + 2 * n + e]).start()
    pump.slot(10)

    @pl.when((c >= 1) & (c < nctx - 1))
    def _():
        far_copy.wait_recv()
        kept[1] += far_land[...].astype(f32)

    @pl.when(c >= 1)
    def _():
        out_buf[1] = scatters[1].total(kept[1]).astype(bf16)
        mid_copy.start()
        scatters[1].close()

    base = locals_.start(d_middle, kept.at[1])
    hidden_load = locals_.start(hidden, out_buf.at[2])
    scatter(scatters[0], 0, all_part)
    for n in range(2):
        rows_of = gkv[half_at(s, n, 256), :].astype(bf16)
        got = first_dot(rowbuf[:, half_at(s, n, 256)], dqp[...]).astype(bf16)
        for e in range(2):
            at = slice(e * 128, e * 128 + 128)
            own[LATE + 2 * n + e] = rows_of[at]
            own[LATE + 4 + 2 * n + e] = got[at]
    for u in range(LATE - 4, LATE):
        pump.second(u)
        pump.third(u - 4)
    pump.third(LATE - 4)
    pump.third(LATE - 3)
    pl.loop(0, LATE - 8)(pump.fourth)

    def finish_rows():
        @pl.when(c < nctx - 1)
        def _():
            mid_copy.wait_recv()
            kept[0] += mid_land[...].astype(f32)

        kept[0] = scatters[0].total(kept[0])
        locals_.wait(hidden_load)
        locals_.wait(base)
        x = out_buf[2].astype(f32)
        r = lax.rsqrt(jnp.mean(x * x, axis=-1, keepdims=True) + norm_eps)
        d_in = kept[0]
        gsum[0:1, :] = jnp.sum(d_in * x * r, axis=0, keepdims=True)
        scaled = d_in * gains[0:1, :]
        inner = jnp.mean(scaled * x, axis=-1, keepdims=True)
        kept[1] += r * scaled - x * (r * r * r) * inner
        locals_.start(kept.at[1], hidden_grad)

    swaps = [
        links.copy(gsum, gland.at[n], device)
        for n, device in enumerate((side, across, mate, near, opposite))
    ]

    def swap(n):
        if n > 0:
            swaps[n - 1].wait()
            gsum[...] += gland[n - 1]
        if n < 5:
            swaps[n].start()

    for n, u in enumerate(range(LATE, UNITS)):
        pump.first(u)
        if n >= 1:
            pump.second(u - 1)
        pump.third(u - 2)
        if n == 3:
            finish_rows()
        if n >= 3:
            swap(n - 3)
    pump.second(UNITS - 1)
    pump.third(UNITS - 2)
    swap(8 - 3)
    pump.third(UNITS - 1)
    for n in range(9 - 3, 6):
        swap(n)
    locals_.start(gsum, gains_out)
    scatters[0].close()

    @pl.when(c >= 2)
    def _():
        far_copy.wait_send()

    @pl.when(c >= 1)
    def _():
        mid_copy.wait_send()

    @pl.loop(MATED, EARLY)
    def _(u):
        pump.to_mate(u, give.at[u - MATED]).wait_send()

    @pl.loop(EARLY, UNITS)
    def _(u):
        pump.to_mate(u, late_give.at[u - EARLY]).wait_send()

    pl.loop(LATE - 8, UNITS)(pump.fourth)
    pump.close()
    locals_.finish()


def backward_call(vmem_args, any_args):
    hidden = any_args[0]
    part, width = hidden.shape
    block = 4 * part
    f32, bf16 = jnp.float32, jnp.bfloat16
    shape = jax.ShapeDtypeStruct
    outs = (
        shape((part, width), bf16),
        shape((part, width), f32),
        shape((8, width), f32),
        shape((UNITS, 128, 512), bf16),
    )
    tile = pltpu.VMEM((part, width), bf16)
    units = pltpu.VMEM((UNITS, 128, 512), bf16)
    return pl.pallas_call(
        backward_kernel,
        name="backward",
        out_shape=outs,
        in_specs=[VMEM_SPEC] * 3 + [ANY_SPEC] * len(any_args),
        out_specs=[ANY_SPEC] * len(outs),
        scratch_shapes=[
            pltpu.VMEM((2, 2, block, 256), bf16),
            pltpu.VMEM((2, 2, block, 256), bf16),
            pltpu.VMEM((block, 256), f32),
            pltpu.VMEM((block, HEAD_SIZE), f32),
            pltpu.VMEM((block, HEAD_SIZE), f32),
            pltpu.VMEM((block, width), bf16),
            pltpu.VMEM((4, block, HEAD_SIZE), f32),
            pltpu.VMEM((2, HEAD_SIZE, block), f32),
            pltpu.VMEM((2, HEAD_SIZE, block), f32),
            pltpu.VMEM((block, 512), bf16),
            pltpu.VMEM((block, 512), bf16),
            pltpu.VMEM((width, 512), f32),
            pltpu.VMEM((2, part, width), f32),
            pltpu.VMEM((2, 6, part, width), bf16),
            units,
            pltpu.VMEM((UNITS - MATED, 128, 512), bf16),
            units,
            units,
            pltpu.VMEM((UNITS - EARLY, 128, 512), bf16),
            tile, tile,
            pltpu.VMEM((4, part, width), bf16),
            pltpu.VMEM((4, block, 256), bf16),
            pltpu.VMEM((block, 512), f32),
            pltpu.VMEM((width, 1024), bf16),
            pltpu.VMEM((8, width), f32),
            pltpu.VMEM((5, 8, width), f32),
            pltpu.SemaphoreType.DMA((22,)),
            pltpu.SemaphoreType.DMA((22,)),
            pltpu.SemaphoreType.DMA((4 * UNITS,)),
            pltpu.SemaphoreType.DMA((4 * UNITS,)),
            pltpu.SemaphoreType.DMA((UNITS,)),
            pltpu.SemaphoreType.DMA((20,)),
            pltpu.SemaphoreType.DMA((18,)),
        ],
        compiler_params=pltpu.CompilerParams(
            collective_id=2, has_side_effects=True, vmem_limit_bytes=60 << 20
        ),
    )(*vmem_args, *any_args)


def result_kernel(
    chunks_in, gains, grad_in, hidden_in,
    grad_out, hidden_out, attn, wq, wk, wv, q_gain, k_gain, wo, mlp, wg, wu, wd,
    buf, q, k, v, o, gate, up, down, grad, hidden, inside, outside,
):
    shard = lax.axis_index(SHARD_AXIS)
    count = buf.shape[0]
    whole = [
        pltpu.make_async_copy(grad_in, grad, inside.at[count]),
        pltpu.make_async_copy(hidden_in, hidden, inside.at[count + 1]),
    ]
    loads = [pltpu.make_async_copy(chunks_in.at[n], buf.at[n], inside.at[n]) for n in range(count)]
    for copy in whole + loads:
        copy.start()
    stores = []

    def put(n, ref, out, row, lanes):
        at = (slice(row, row + 256), lanes)
        stores.append(pltpu.make_async_copy(ref.at[at], out.at[at], outside.at[len(stores)]))
        stores[-1].start()

    for copy in whole:
        copy.wait()
    for n, (ref, out) in enumerate(((grad, grad_out), (hidden, hidden_out))):
        whole[n] = pltpu.make_async_copy(ref, out, outside.at[count + n])
        whole[n].start()
    for n in range(count):
        loads[n].wait()
        values = buf[n].astype(jnp.float32)
        every = slice(0, 512)
        if n < 3:
            down[n * 256 : n * 256 + 256, :] = values
            put(n, down, wd, n * 256, every)
        elif n < 9:
            ref, out, j = (gate, wg, n - 3) if n < 6 else (up, wu, n - 6)
            lanes = slice(j * 256, j * 256 + 256)
            ref[0:256, lanes] = values[:, 0:256]
            ref[256:512, lanes] = values[:, 256:512]
            at = (slice(0, 512), lanes)
            stores.append(pltpu.make_async_copy(ref.at[at], out.at[at], outside.at[len(stores)]))
            stores[-1].start()
        elif n < 11:
            o[(n - 9) * 256 : (n - 8) * 256, :] = values
            put(n, o, wo, (n - 9) * 256, every)
        elif n < 13:
            row = (n - 11) * 256
            k[row : row + 256, :] = values[:, 0:256]
            v[row : row + 256, :] = values[:, 256:512]
        else:
            q[(n - 13) * 256 : (n - 12) * 256, :] = values
            put(n, q, wq, (n - 13) * 256, every)
    for ref, out in ((k, wk), (v, wv)):
        stores.append(pltpu.make_async_copy(ref, out, outside.at[len(stores)]))
        stores[-1].start()
    wide, small = attn.shape[1], q_gain.shape[1]
    first = shard == 0
    attn[...] = jnp.where(first, gains[0:1, 0:wide], gains[0:1, wide : 2 * wide])
    mlp[...] = jnp.where(first, gains[1:2, 0:wide], gains[1:2, wide : 2 * wide])
    q_gain[...] = jnp.where(first, gains[2:3, 0:small], gains[2:3, small : 2 * small])
    k_gain[...] = jnp.where(first, gains[3:4, 0:small], gains[3:4, small : 2 * small])
    for copy in stores + whole:
        copy.wait()


def result_call(chunks, gains, grad_hidden, out_hidden):
    part, width = grad_hidden.shape
    f32 = jnp.float32
    shape = jax.ShapeDtypeStruct
    half = width // 2
    q, k, v, o = (half, 512), (half, 256), (half, 256), (512, half)
    gate, up, down = (half, 768), (half, 768), (768, half)
    sizes = [q, k, v, (1, 64), (1, 64), o, (1, half), gate, up, down]
    outs = [shape((part, width), f32), shape((part, width), out_hidden.dtype), shape((1, half), f32)]
    outs += [shape(z, f32) for z in sizes]
    specs = [ANY_SPEC] * 2 + [VMEM_SPEC] + [ANY_SPEC] * 3 + [VMEM_SPEC] * 2 + [ANY_SPEC, VMEM_SPEC]
    return pl.pallas_call(
        result_kernel,
        name="result",
        out_shape=outs,
        in_specs=[ANY_SPEC, VMEM_SPEC, ANY_SPEC, ANY_SPEC],
        out_specs=specs + [ANY_SPEC] * 3,
        scratch_shapes=[pltpu.VMEM((CHUNKS, 256, 512), jnp.bfloat16)]
        + [pltpu.VMEM(z, f32) for z in (q, k, v, o, gate, up, down)]
        + [pltpu.VMEM((part, width), f32), pltpu.VMEM((part, width), out_hidden.dtype)]
        + [pltpu.SemaphoreType.DMA((CHUNKS + 2,)), pltpu.SemaphoreType.DMA((CHUNKS + 2,))],
        compiler_params=pltpu.CompilerParams(vmem_limit_bytes=60 << 20),
    )(chunks, gains, grad_hidden, out_hidden)


def fast_device(
    hidden,
    segments,
    cotangent,
    attn_gain,
    w_query,
    key_weight_matrix,
    value_weight_matrix,
    query_gain,
    key_gain,
    mixer_exit_coefficients,
    mlp_gain,
    w_gate,
    w_up,
    w_down,
):
    gains_own, at = 0, 0
    every = (attn_gain, mlp_gain, query_gain, key_gain)
    total = sum(gain.shape[0] for gain in every)
    for gain in every:
        gains_own += jnp.pad(gain[None], ((0, 0), (at, total - at - gain.shape[0])))
        at += gain.shape[0]
    exponents = 2.0 * (np.arange(HEAD_SIZE) % (HEAD_SIZE // 2)) / HEAD_SIZE
    rates = np.power(rope_base, -exponents).astype(np.float32)[None]
    labels = segments.reshape(-1, HEAD_SIZE)
    (gains, rows, q_proj, k_proj, query, keys, values, cosine, sine, attended, low, wqkv, crows,
     wo_got, wg_got, wu_got) = forward_call(
        hidden[0], cotangent[0], gains_own, labels, jnp.asarray(rates), w_query, key_weight_matrix,
        value_weight_matrix, mixer_exit_coefficients, w_gate, w_up,
    )
    def units(chunks, count):
        return chunks.reshape(count, 128, 512)

    d_middle, mlp_gain_grad, brow, own, give, parts, out_own = mlp_call(
        (low, hidden[0], gains),
        (crows, mixer_exit_coefficients, wo_got, w_gate, wg_got, w_up, wu_got, w_down),
    )
    out_hidden, grad_hidden, sums, chunks = backward_call(
        (query, gains, mlp_gain_grad),
        (hidden[0], brow, low, attended, mixer_exit_coefficients, wo_got, d_middle, q_proj, wqkv, units(own, EARLY), units(give, EARLY - MATED),
         parts, out_own, keys, values, k_proj, cosine, sine, rows),
    )
    (grad_hidden, out_hidden, attn, wq, wk, wv, q_gain, k_gain, wo, mlp, wg, wu, wd) = result_call(
        chunks.reshape(CHUNKS, 256, 512), sums, grad_hidden, out_hidden
    )
    return (
        out_hidden[None], grad_hidden[None], attn[0], wq, wk, wv, q_gain[0], k_gain[0], wo, mlp[0],
        wg, wu, wd,
    )


def per_device(
    hidden,
    segments,
    cotangent,
    attn_gain,
    w_query,
    key_weight_matrix,
    value_weight_matrix,
    query_gain,
    key_gain,
    mixer_exit_coefficients,
    mlp_gain,
    w_gate,
    w_up,
    w_down,
):
    collected_rows = (
        lax.all_gather(attn_gain, SHARD_AXIS, axis=0, tiled=True),
        lax.all_gather(w_query, SHARD_AXIS, axis=0, tiled=True),
        lax.all_gather(key_weight_matrix, SHARD_AXIS, axis=0, tiled=True),
        lax.all_gather(value_weight_matrix, SHARD_AXIS, axis=0, tiled=True),
        lax.all_gather(query_gain, SHARD_AXIS, axis=0, tiled=True),
        lax.all_gather(key_gain, SHARD_AXIS, axis=0, tiled=True),
        lax.all_gather(mixer_exit_coefficients, SHARD_AXIS, axis=1, tiled=True),
        lax.all_gather(mlp_gain, SHARD_AXIS, axis=0, tiled=True),
        lax.all_gather(w_gate, SHARD_AXIS, axis=0, tiled=True),
        lax.all_gather(w_up, SHARD_AXIS, axis=0, tiled=True),
        lax.all_gather(w_down, SHARD_AXIS, axis=1, tiled=True),
    )
    gain_attn = collected_rows[0].astype(jnp.float32)
    gain_query = collected_rows[4].astype(jnp.float32)
    gain_key = collected_rows[5].astype(jnp.float32)
    gain_mlp = collected_rows[7].astype(jnp.float32)
    seq_count = hidden.shape[0]
    block_rows = hidden.shape[1] * lax.axis_size(TP_AXIS)
    seq_length = segments.shape[1]
    ctx_index = lax.axis_index(CTX_AXIS)
    heads_local = w_query.shape[1] // HEAD_SIZE
    kv_local = key_weight_matrix.shape[1] // HEAD_SIZE
    query_group_width = heads_local // kv_local
    score_scale = HEAD_SIZE ** (-0.5)
    block_start = ctx_index * block_rows
    query_pos = block_start + jnp.arange(block_rows, dtype=jnp.int32)
    query_seg = lax.dynamic_slice_in_dim(segments, block_start, block_rows, 1)
    positions = lax.dynamic_slice_in_dim(doc_positions(segments), block_start, block_rows, 1)
    cosine, sine_part = rope_tables(positions)

    def counting_keys(key_first, step_rows):
        early = key_first <= block_start + block_rows - 1
        last_seg = lax.dynamic_slice_in_dim(segments, key_first + step_rows - 1, 1, 1)[:, 0]
        return early & jnp.any(last_seg >= query_seg[:, 0])

    inputs = hidden.astype(jnp.float32)
    scale_one = rms_scale(inputs)
    attention_input = (inputs * scale_one * gain_attn).astype(jnp.bfloat16)
    attention_rows = tp_rows(attention_input)
    q_proj = jnp.einsum(
        "zjr,rm->zjm", attention_rows, collected_rows[1], preferred_element_type=jnp.float32
    ).reshape(seq_count, block_rows, heads_local, HEAD_SIZE)
    key_projected = jnp.einsum(
        "zjr,rm->zjm", attention_rows, collected_rows[2], preferred_element_type=jnp.float32
    ).reshape(seq_count, block_rows, kv_local, HEAD_SIZE)
    value_projected = jnp.einsum(
        "zjr,rm->zjm", attention_rows, collected_rows[3], preferred_element_type=jnp.float32
    )
    q_scale = rms_scale(q_proj)
    k_scale = rms_scale(key_projected)
    query_rows_input = (
        rotate(q_proj * q_scale * gain_query, cosine, sine_part)
        .astype(jnp.bfloat16)
        .reshape(seq_count, block_rows, kv_local, query_group_width, HEAD_SIZE)
    )
    keys = rotate(key_projected * k_scale * gain_key, cosine, sine_part).astype(jnp.bfloat16)
    values = value_projected.astype(jnp.bfloat16).reshape(
        seq_count, block_rows, kv_local, HEAD_SIZE
    )
    stat_shape = (seq_count, kv_local, query_group_width, block_rows)
    start_state = (
        jnp.full(stat_shape, masked_fill, jnp.float32),
        jnp.zeros(stat_shape, jnp.float32),
        jnp.zeros(stat_shape + (HEAD_SIZE,), jnp.float32),
    )
    piece_keys = lax.all_gather(keys, CTX_AXIS, axis=1, tiled=True)
    piece_values = lax.all_gather(values, CTX_AXIS, axis=1, tiled=True)
    piece_rows = piece_keys.shape[1]
    step_rows = math.gcd(piece_rows, 1024)

    def attend_one_step(number, loop_state):
        offset = number * step_rows
        key_first = offset

        def attend_compute(state):
            row_max, row_total, summed = state
            key_part = lax.dynamic_slice_in_dim(piece_keys, offset, step_rows, 1)
            value_part = lax.dynamic_slice_in_dim(piece_values, offset, step_rows, 1)
            allowed = key_block(segments, key_first, step_rows, query_pos, query_seg)
            scores = (
                jnp.einsum(
                    "sqhgd,skhd->shgqk",
                    query_rows_input,
                    key_part,
                    preferred_element_type=jnp.float32,
                )
                * score_scale
            )
            masked = jnp.where(allowed, scores, masked_fill)
            new_max = jnp.maximum(row_max, jnp.max(masked, axis=-1))
            weights = jnp.where(allowed, jnp.exp(masked - new_max[..., None]), 0.0)
            decay_factor = jnp.exp(row_max - new_max)
            row_total = row_total * decay_factor + jnp.sum(weights, axis=-1)
            summed = summed * decay_factor[..., None] + jnp.einsum(
                "shgqk,skhd->shgqd",
                weights.astype(jnp.bfloat16),
                value_part,
                preferred_element_type=jnp.float32,
            )
            return (new_max, row_total, summed)

        return lax.cond(counting_keys(key_first, step_rows), attend_compute, keep_state, loop_state)

    row_max, row_total, summed = lax.fori_loop(
        0, piece_rows // step_rows, attend_one_step, start_state
    )
    attended = summed / row_total[..., None]
    log_total = row_max + jnp.log(row_total)
    attended_reduced_copy = (
        attended.transpose(0, 3, 1, 2, 4)
        .reshape(seq_count, block_rows, heads_local * HEAD_SIZE)
        .astype(jnp.bfloat16)
    )
    branch = tp_total(
        jnp.einsum(
            "vkq,qy->vky",
            attended_reduced_copy,
            collected_rows[6],
            preferred_element_type=jnp.float32,
        )
    )
    middle = inputs + branch
    scale_two = rms_scale(middle)
    mlp_in = (middle * scale_two * gain_mlp).astype(jnp.bfloat16)
    mlp_rows = tp_rows(mlp_in)
    gate = jnp.einsum(
        "snd,df->snf", mlp_rows, collected_rows[8], preferred_element_type=jnp.float32
    )
    upward = jnp.einsum(
        "snd,df->snf", mlp_rows, collected_rows[9], preferred_element_type=jnp.float32
    )
    activated = (jax.nn.silu(gate) * upward).astype(jnp.bfloat16)
    out_hidden = (
        middle
        + tp_total(
            jnp.einsum(
                "snf,fd->snd", activated, collected_rows[10], preferred_element_type=jnp.float32
            )
        )
    ).astype(jnp.bfloat16)
    again = (
        lax.all_gather(attn_gain, SHARD_AXIS, axis=0, tiled=True),
        lax.all_gather(w_query, SHARD_AXIS, axis=0, tiled=True),
        lax.all_gather(key_weight_matrix, SHARD_AXIS, axis=0, tiled=True),
        lax.all_gather(value_weight_matrix, SHARD_AXIS, axis=0, tiled=True),
        lax.all_gather(query_gain, SHARD_AXIS, axis=0, tiled=True),
        lax.all_gather(key_gain, SHARD_AXIS, axis=0, tiled=True),
        lax.all_gather(mixer_exit_coefficients, SHARD_AXIS, axis=1, tiled=True),
        lax.all_gather(mlp_gain, SHARD_AXIS, axis=0, tiled=True),
        lax.all_gather(w_gate, SHARD_AXIS, axis=0, tiled=True),
        lax.all_gather(w_up, SHARD_AXIS, axis=0, tiled=True),
        lax.all_gather(w_down, SHARD_AXIS, axis=1, tiled=True),
    )
    query_backward = again[1]
    lookup_pullback = again[2]
    value_backward = again[3]
    output_backward = again[6]
    back_gate = again[8]
    back_up = again[9]
    back_down = again[10]
    d_out = cotangent.astype(jnp.float32)
    d_rows = tp_rows(cotangent)
    grad_down = jnp.einsum("snf,snd->fd", activated, d_rows, preferred_element_type=jnp.float32)
    d_act = jnp.einsum("snd,fd->snf", d_rows, back_down, preferred_element_type=jnp.float32)
    sigmoid_gate = jax.nn.sigmoid(gate)
    d_upward = (d_act * jax.nn.silu(gate)).astype(jnp.bfloat16)
    d_gate = (d_act * upward * sigmoid_gate * (1.0 + gate * (1.0 - sigmoid_gate))).astype(
        jnp.bfloat16
    )
    grad_gate = jnp.einsum("snd,snf->df", mlp_rows, d_gate, preferred_element_type=jnp.float32)
    grad_up = jnp.einsum("snd,snf->df", mlp_rows, d_upward, preferred_element_type=jnp.float32)
    d_mlp_in = tp_total(
        jnp.einsum("snf,df->snd", d_gate, back_gate, preferred_element_type=jnp.float32)
        + jnp.einsum("snf,df->snd", d_upward, back_up, preferred_element_type=jnp.float32)
    )
    grad_mlp_gain = jnp.sum(d_mlp_in * middle * scale_two, axis=(0, 1))
    d_middle = d_out + rms_back(d_mlp_in, middle, scale_two, gain_mlp)
    d_branch = d_middle.astype(jnp.bfloat16)
    residual_branch_rows = tp_rows(d_branch)
    result_cotangent = jnp.einsum(
        "xbj,xbk->jk",
        attended_reduced_copy,
        residual_branch_rows,
        preferred_element_type=jnp.float32,
    )
    d_attended = (
        jnp.einsum(
            "miv,cv->mic", residual_branch_rows, output_backward, preferred_element_type=jnp.float32
        )
        .astype(jnp.bfloat16)
        .reshape(seq_count, block_rows, kv_local, query_group_width, HEAD_SIZE)
    )
    delta = jnp.sum(d_attended.astype(jnp.float32).transpose(0, 2, 3, 1, 4) * attended, axis=-1)
    query_zeros = jnp.zeros(
        (seq_count, block_rows, kv_local, query_group_width, HEAD_SIZE), jnp.float32
    )
    back_state = (
        query_zeros,
        jnp.zeros((seq_count, seq_length, kv_local, HEAD_SIZE), jnp.float32),
        jnp.zeros((seq_count, seq_length, kv_local, HEAD_SIZE), jnp.float32),
    )
    back_piece_keys = lax.all_gather(keys, CTX_AXIS, axis=1, tiled=True)
    back_piece_values = lax.all_gather(values, CTX_AXIS, axis=1, tiled=True)
    piece_rows = back_piece_keys.shape[1]
    back_step_rows = math.gcd(piece_rows, 1024)

    def back_one_step(number, loop_state):
        offset = number * back_step_rows
        key_first = offset
        write_at = offset

        def back_compute(state):
            d_query, d_keys, d_values = state
            key_part = lax.dynamic_slice_in_dim(back_piece_keys, offset, back_step_rows, 1)
            value_part = lax.dynamic_slice_in_dim(back_piece_values, offset, back_step_rows, 1)
            allowed = key_block(segments, key_first, back_step_rows, query_pos, query_seg)
            scores = (
                jnp.einsum(
                    "sqhgd,skhd->shgqk",
                    query_rows_input,
                    key_part,
                    preferred_element_type=jnp.float32,
                )
                * score_scale
            )
            probs = jnp.where(allowed, jnp.exp(scores - log_total[..., None]), 0.0)
            d_probs = jnp.einsum(
                "sqhgd,skhd->shgqk", d_attended, value_part, preferred_element_type=jnp.float32
            )
            d_scores = (probs * (d_probs - delta[..., None])).astype(jnp.bfloat16)
            d_query = d_query + jnp.einsum(
                "shgqk,skhd->sqhgd", d_scores, key_part, preferred_element_type=jnp.float32
            )
            key_grad = jnp.einsum(
                "shgqk,sqhgd->skhd", d_scores, query_rows_input, preferred_element_type=jnp.float32
            )
            value_grad = jnp.einsum(
                "shgqk,sqhgd->skhd",
                probs.astype(jnp.bfloat16),
                d_attended,
                preferred_element_type=jnp.float32,
            )
            d_keys = lax.dynamic_update_slice_in_dim(
                d_keys,
                lax.dynamic_slice_in_dim(d_keys, write_at, back_step_rows, 1) + key_grad,
                write_at,
                1,
            )
            d_values = lax.dynamic_update_slice_in_dim(
                d_values,
                lax.dynamic_slice_in_dim(d_values, write_at, back_step_rows, 1) + value_grad,
                write_at,
                1,
            )
            return (d_query, d_keys, d_values)

        return lax.cond(
            counting_keys(key_first, back_step_rows), back_compute, keep_state, loop_state
        )

    d_query, d_keys, d_values = lax.fori_loop(
        0, piece_rows // back_step_rows, back_one_step, back_state
    )
    own_keys, own_values = (
        lax.psum_scatter(
            d_keys.astype(jnp.bfloat16), CTX_AXIS, scatter_dimension=1, tiled=True
        ).astype(jnp.float32),
        lax.psum_scatter(
            d_values.astype(jnp.bfloat16), CTX_AXIS, scatter_dimension=1, tiled=True
        ).astype(jnp.float32),
    )
    q_normed = rotate_back(
        d_query.reshape(seq_count, block_rows, heads_local, HEAD_SIZE) * score_scale,
        cosine,
        sine_part,
    )
    grad_query_gain = jnp.sum(q_normed * q_proj * q_scale, axis=(0, 1, 2))
    query_projection_gradient = (
        rms_back(q_normed, q_proj, q_scale, gain_query)
        .astype(jnp.bfloat16)
        .reshape(seq_count, block_rows, heads_local * HEAD_SIZE)
    )
    k_normed = rotate_back(own_keys * score_scale, cosine, sine_part)
    grad_key_gain = jnp.sum(k_normed * key_projected * k_scale, axis=(0, 1, 2))
    lookup_map_derivative = (
        rms_back(k_normed, key_projected, k_scale, gain_key)
        .astype(jnp.bfloat16)
        .reshape(seq_count, block_rows, kv_local * HEAD_SIZE)
    )
    value_projection_gradient = own_values.astype(jnp.bfloat16).reshape(
        seq_count, block_rows, kv_local * HEAD_SIZE
    )
    query_gradient_rows = jnp.einsum(
        "zqr,zqa->ra", attention_rows, query_projection_gradient, preferred_element_type=jnp.float32
    )
    key_gradient_rows = jnp.einsum(
        "zqr,zqa->ra", attention_rows, lookup_map_derivative, preferred_element_type=jnp.float32
    )
    value_gradient_rows = jnp.einsum(
        "zqr,zqa->ra", attention_rows, value_projection_gradient, preferred_element_type=jnp.float32
    )
    d_attn_in = tp_total(
        jnp.einsum(
            "wtl,al->wta",
            query_projection_gradient,
            query_backward,
            preferred_element_type=jnp.float32,
        )
        + jnp.einsum(
            "wtl,al->wta",
            lookup_map_derivative,
            lookup_pullback,
            preferred_element_type=jnp.float32,
        )
        + jnp.einsum(
            "wtl,al->wta",
            value_projection_gradient,
            value_backward,
            preferred_element_type=jnp.float32,
        )
    )
    grad_attn_gain = jnp.sum(d_attn_in * inputs * scale_one, axis=(0, 1))
    grad_hidden = d_middle + rms_back(d_attn_in, inputs, scale_one, gain_attn)
    reduced = (
        lax.psum_scatter(
            grad_attn_gain.astype(jnp.bfloat16), SHARD_AXIS, scatter_dimension=0, tiled=True
        ).astype(jnp.float32),
        lax.psum_scatter(
            query_gradient_rows.astype(jnp.bfloat16), SHARD_AXIS, scatter_dimension=0, tiled=True
        ).astype(jnp.float32),
        lax.psum_scatter(
            key_gradient_rows.astype(jnp.bfloat16), SHARD_AXIS, scatter_dimension=0, tiled=True
        ).astype(jnp.float32),
        lax.psum_scatter(
            value_gradient_rows.astype(jnp.bfloat16), SHARD_AXIS, scatter_dimension=0, tiled=True
        ).astype(jnp.float32),
        lax.psum_scatter(
            grad_query_gain.astype(jnp.bfloat16), SHARD_AXIS, scatter_dimension=0, tiled=True
        ).astype(jnp.float32),
        lax.psum_scatter(
            grad_key_gain.astype(jnp.bfloat16), SHARD_AXIS, scatter_dimension=0, tiled=True
        ).astype(jnp.float32),
        lax.psum_scatter(
            result_cotangent.astype(jnp.bfloat16), SHARD_AXIS, scatter_dimension=1, tiled=True
        ).astype(jnp.float32),
        lax.psum_scatter(
            grad_mlp_gain.astype(jnp.bfloat16), SHARD_AXIS, scatter_dimension=0, tiled=True
        ).astype(jnp.float32),
        lax.psum_scatter(
            grad_gate.astype(jnp.bfloat16), SHARD_AXIS, scatter_dimension=0, tiled=True
        ).astype(jnp.float32),
        lax.psum_scatter(
            grad_up.astype(jnp.bfloat16), SHARD_AXIS, scatter_dimension=0, tiled=True
        ).astype(jnp.float32),
        lax.psum_scatter(
            grad_down.astype(jnp.bfloat16), SHARD_AXIS, scatter_dimension=1, tiled=True
        ).astype(jnp.float32),
    )
    matrices = (
        lax.psum(reduced[1].astype(jnp.bfloat16), CTX_AXIS).astype(jnp.float32),
        lax.psum(reduced[2].astype(jnp.bfloat16), CTX_AXIS).astype(jnp.float32),
        lax.psum(reduced[3].astype(jnp.bfloat16), CTX_AXIS).astype(jnp.float32),
        lax.psum(reduced[6].astype(jnp.bfloat16), CTX_AXIS).astype(jnp.float32),
        lax.psum(reduced[8].astype(jnp.bfloat16), CTX_AXIS).astype(jnp.float32),
        lax.psum(reduced[9].astype(jnp.bfloat16), CTX_AXIS).astype(jnp.float32),
        lax.psum(reduced[10].astype(jnp.bfloat16), CTX_AXIS).astype(jnp.float32),
    )
    gains = lax.psum((reduced[0], reduced[4], reduced[5], reduced[7]), (CTX_AXIS, TP_AXIS))
    return (
        out_hidden,
        grad_hidden,
        gains[0],
        matrices[0],
        matrices[1],
        matrices[2],
        gains[1],
        gains[2],
        matrices[3],
        gains[3],
        matrices[4],
        matrices[5],
        matrices[6],
    )


def solution(mesh):
    in_specs = (
        P(SHARD_AXIS, (CTX_AXIS, TP_AXIS), None),
        P(SHARD_AXIS, None),
        P(SHARD_AXIS, (CTX_AXIS, TP_AXIS), None),
        P(SHARD_AXIS),
        P(SHARD_AXIS, TP_AXIS),
        P(SHARD_AXIS, TP_AXIS),
        P(SHARD_AXIS, TP_AXIS),
        P(SHARD_AXIS),
        P(SHARD_AXIS),
        P(TP_AXIS, SHARD_AXIS),
        P(SHARD_AXIS),
        P(SHARD_AXIS, TP_AXIS),
        P(SHARD_AXIS, TP_AXIS),
        P(TP_AXIS, SHARD_AXIS),
    )
    out_specs = (
        P(SHARD_AXIS, (CTX_AXIS, TP_AXIS), None),
        P(SHARD_AXIS, (CTX_AXIS, TP_AXIS), None),
        P(SHARD_AXIS),
        P(SHARD_AXIS, TP_AXIS),
        P(SHARD_AXIS, TP_AXIS),
        P(SHARD_AXIS, TP_AXIS),
        P(SHARD_AXIS),
        P(SHARD_AXIS),
        P(TP_AXIS, SHARD_AXIS),
        P(SHARD_AXIS),
        P(SHARD_AXIS, TP_AXIS),
        P(SHARD_AXIS, TP_AXIS),
        P(TP_AXIS, SHARD_AXIS),
    )
    shape = mesh.shape
    fast = shape[SHARD_AXIS] == 2 and shape[CTX_AXIS] == 4 and shape[TP_AXIS] == 4
    return jax.shard_map(
        fast_device if fast else per_device, mesh=mesh, in_specs=in_specs, out_specs=out_specs, check_vma=False
    )
```

profile of v0, /device:TPU:0, one launch (start us, length us, event | category | flops | bytes accessed | tf_op | source)
XLA Modules:
  0.0 272.3 jit_solution(87003384893026139)
XLA Ops:
  0.6 0.7 broadcast_in_dim.18
  1.3 0.7 broadcast_in_dim.19
  2.0 1.3 pad_add_fusion.gains_own
  3.3 59.1 %forward.1 = (f32[8,1024]{1,0:T(8,128)}, bf16[3,1024,1024]{2,1,0:T(8,128)(2,1)}, f32[1024,512]{1,0:T(8,128)}, f32[3,1024,256]{2,1,0:T(8,128)}, bf16[4,1024,256]{...) custom-call(bf16[256,1024]{1,0:T(8,128)(2,1)} %bitcast.14, ...), custom_call_target="tpu_custom_call" | custom-call | tf_op jit(solution)/shard_map/forward/pallas_call | solution.py:558
  62.5 56.2 %mlp.1 = (f32[256,1024]{1,0:T(8,128)}, f32[8,1024]{1,0:T(8,128)}, bf16[256,1024]{1,0:T(8,128)(2,1)}, bf16[9,256,512]{2,1,0:T(8,128)(2,1)}, bf16[7,256,512]{2,1,0...) custom-call(bf16[1024,512]{1,0:T(8,128)(2,1)} %get-tuple-element.55.low, bf16[256,1024]{1,0:T(8,128)(2,1)} %bitcast.15, ...), custom_call_target="tpu_custom_call" | custom-call | tf_op jit(solution)/shard_map/mlp/pallas_call | solution.py:843
  118.7 146.8 %backward.1 = (bf16[256,1024]{1,0:T(8,128)(2,1)}, f32[256,1024]{1,0:T(8,128)}, f32[8,1024]{1,0:T(8,128)}, bf16[30,128,512]{2,1,0:T(8,128)(2,1)}) custom-call(bf16[4,1024,256]{2,1,0:T(8,128)(2,1)} %get-tuple-element.53.query, f32[8,1024]{1,0:T(8,128)} %get-tuple-element.54.gains, f32[8,1024]{1,0:T(8,128)} %get-tuple-element.60.mlp_gain_grad, ...), custom_call_target="tpu_custom_call" | custom-call | tf_op jit(solution)/shard_map/backward/pallas_call | solution.py:1427
  265.5 6.6 %result.1 = (f32[256,1024]{1,0:T(8,128)}, bf16[256,1024]{1,0:T(8,128)(2,1)}, f32[1,512]{1,0:T(1,128)}, f32[512,512]{1,0:T(8,128)}, f32[512,256]{1,0:T(8,128)}, /...) custom-call(bf16[15,256,512]{2,1,0:T(8,128)(2,1)} %bitcast.17, ...), custom_call_target="tpu_custom_call" | custom-call | tf_op jit(solution)/shard_map/result/pallas_call | solution.py:1549
where the time goes:
time: 273 us; the launch traced here: 272 us
  Pallas kernels  269 us (99%)
    pallas_call x1, Pallas kernels, backward_call(): pl.pallas_call(backward_kernel, name='backward', out_shape=outs, in_specs...  147 us
    pallas_call x1, Pallas kernels, forward_call(): pl.pallas_call(forward_kernel, name='forward', out_shape=outs, in_specs=[...  59.1 us
    pallas_call x1, Pallas kernels, mlp_call(): pl.pallas_call(mlp_kernel, name='mlp', out_shape=outs, in_specs=[VMEM_SPE...  56.2 us
    pallas_call x1, Pallas kernels, result_call(): pl.pallas_call(result_kernel, name='result', out_shape=outs, in_specs=[AN...  6.6 us

commit v1 on v0

--- a/solution.py
+++ b/solution.py
@@ -161,7 +161,7 @@
 
 
 def forward_kernel(
-    hidden, cotangent, gains_own, segments, rates, wq, wk, wv, wo, wg, wu,
+    hidden, cotangent, attn_gain, mlp_gain, query_gain, key_gain, segments, rates, wq, wk, wv, wo, wg, wu,
     gains_out, rows_out, q_out, k_out, query_out, keys_out, values_out, cos_out, sin_out,
     attended_out, low_out, wqkv_out, crows_out, wo_out, wg_out, wu_out,
     gains, raw, rows, wqkv, q_proj, k_proj, qaug, kaug, vaug, cosine, sine, acc, low, crows,
@@ -177,17 +177,15 @@
     pair = {CTX_AXIS: c ^ 1}
     nxt, prv = {CTX_AXIS: lax.rem(c + 1, nctx)}, {CTX_AXIS: lax.rem(c + nctx - 1, nctx)}
     gains_in[...] = jnp.zeros(gains_in.shape, f32)
-    for row in range(2):
-        own_gain = gains_own[:, row * half : row * half + half].astype(f32)
+    for row, gain in enumerate((attn_gain, mlp_gain)):
+        own_gain = gain[...].astype(f32)[None, :]
         gains_in[row : row + 1, pl.ds(pl.multiple_of(s * half, half), half)] = own_gain
-    small = jnp.broadcast_to(gains_own[:, 2 * half : 2 * half + HEAD_SIZE], (16, HEAD_SIZE))
-    square = (HEAD_SIZE, HEAD_SIZE)
-    source_lane = lax.broadcasted_iota(jnp.int32, square, 0)
-    target_lane = lax.broadcasted_iota(jnp.int32, square, 1) - s * (HEAD_SIZE // 2)
-    for row, first in ((2, 0), (3, HEAD_SIZE // 2)):
-        chosen = (source_lane - first == target_lane) & (source_lane >= first)
-        chosen = chosen & (source_lane < first + HEAD_SIZE // 2)
-        placed = flat_dot(small, jnp.where(chosen, 1.0, 0.0).astype(bf16))
+    small = HEAD_SIZE // 2
+    source_lane = lax.broadcasted_iota(jnp.int32, (small, HEAD_SIZE), 0)
+    target_lane = lax.broadcasted_iota(jnp.int32, (small, HEAD_SIZE), 1) - s * small
+    chosen = jnp.where(source_lane == target_lane, 1.0, 0.0).astype(bf16)
+    for row, gain in ((2, query_gain), (3, key_gain)):
+        placed = flat_dot(jnp.broadcast_to(gain[...][None, :], (16, small)), chosen)
         gains_in[row : row + 1, 0:HEAD_SIZE] = placed[0:1]
     enter([side, across, mate, nxt, prv])
     links, locals_ = Links(send, recv), Locals(local)
@@ -559,7 +557,7 @@
         forward_kernel,
         name="forward",
         out_shape=outs,
-        in_specs=[VMEM_SPEC] * 5 + [ANY_SPEC] * 6,
+        in_specs=[VMEM_SPEC] * 8 + [ANY_SPEC] * 6,
         out_specs=[ANY_SPEC] * len(outs),
         scratch_shapes=[
             pltpu.VMEM((8, width), f32),
@@ -586,7 +584,7 @@
         compiler_params=pltpu.CompilerParams(
             collective_id=0, has_side_effects=True, vmem_limit_bytes=58 << 20
         ),
-    )(hidden, cotangent, gains, segments, rates, wq, wk, wv, wo, wg, wu)
+    )(hidden, cotangent, *gains, segments, rates, wq, wk, wv, wo, wg, wu)
 
 
 class Scatter:
@@ -960,12 +958,12 @@
 
 
 def backward_kernel(
-    query, gains, mlp_gain_grad, hidden, brow_in, low, attended, wo_own, wo_got, d_middle,
+    gains, mlp_gain_grad, query_in, hidden, brow_in, low, attended, wo_own, wo_got, d_middle,
     q_proj_in, wqkv_in, own_in, give, parts, out_own, keys, values, k_proj, cosine, sine, rows,
     hidden_out, hidden_grad, gains_out, sums_out,
     kbuf, vbuf, kpbuf, cosbuf, sinbuf, rowbuf, dq, dk, dv, dkv, dqp, gkv, kept, bufs,
     own, mated, landed, summed, late_give, far_land, mid_land, out_buf,
-    dout, q_proj, wqkv,
+    query, dout, q_proj, wqkv,
     gsum, gland, send, recv, pump_send, pump_recv, pump_local, local, blocksem,
 ):
     s, c, t = lax.axis_index(SHARD_AXIS), lax.axis_index(CTX_AXIS), lax.axis_index(TP_AXIS)
@@ -1048,7 +1046,10 @@
     def _():
         fetch(0)
 
-    late_loads = [locals_.start(q_proj_in, q_proj), locals_.start(wqkv_in, wqkv)]
+    late_loads = [
+        locals_.start(query_in, query), locals_.start(q_proj_in, q_proj),
+        locals_.start(wqkv_in, wqkv),
+    ]
     enter([side, across, mate, near, opposite])
 
     def send_early(first, count):
@@ -1411,7 +1412,7 @@
 
 
 def backward_call(vmem_args, any_args):
-    hidden = any_args[0]
+    hidden = any_args[1]
     part, width = hidden.shape
     block = 4 * part
     f32, bf16 = jnp.float32, jnp.bfloat16
@@ -1428,7 +1429,7 @@
         backward_kernel,
         name="backward",
         out_shape=outs,
-        in_specs=[VMEM_SPEC] * 3 + [ANY_SPEC] * len(any_args),
+        in_specs=[VMEM_SPEC] * 2 + [ANY_SPEC] * len(any_args),
         out_specs=[ANY_SPEC] * len(outs),
         scratch_shapes=[
             pltpu.VMEM((2, 2, block, 256), bf16),
@@ -1453,6 +1454,7 @@
             tile, tile,
             pltpu.VMEM((4, part, width), bf16),
             pltpu.VMEM((4, block, 256), bf16),
+            pltpu.VMEM((4, block, 256), bf16),
             pltpu.VMEM((block, 512), f32),
             pltpu.VMEM((width, 1024), bf16),
             pltpu.VMEM((8, width), f32),
@@ -1462,7 +1464,7 @@
             pltpu.SemaphoreType.DMA((4 * UNITS,)),
             pltpu.SemaphoreType.DMA((4 * UNITS,)),
             pltpu.SemaphoreType.DMA((UNITS,)),
-            pltpu.SemaphoreType.DMA((20,)),
+            pltpu.SemaphoreType.DMA((21,)),
             pltpu.SemaphoreType.DMA((18,)),
         ],
         compiler_params=pltpu.CompilerParams(
@@ -1576,12 +1578,7 @@
     w_up,
     w_down,
 ):
-    gains_own, at = 0, 0
-    every = (attn_gain, mlp_gain, query_gain, key_gain)
-    total = sum(gain.shape[0] for gain in every)
-    for gain in every:
-        gains_own += jnp.pad(gain[None], ((0, 0), (at, total - at - gain.shape[0])))
-        at += gain.shape[0]
+    gains_own = (attn_gain, mlp_gain, query_gain, key_gain)
     exponents = 2.0 * (np.arange(HEAD_SIZE) % (HEAD_SIZE // 2)) / HEAD_SIZE
     rates = np.power(rope_base, -exponents).astype(np.float32)[None]
     labels = segments.reshape(-1, HEAD_SIZE)
@@ -1598,8 +1595,8 @@
         (crows, mixer_exit_coefficients, wo_got, w_gate, wg_got, w_up, wu_got, w_down),
     )
     out_hidden, grad_hidden, sums, chunks = backward_call(
-        (query, gains, mlp_gain_grad),
-        (hidden[0], brow, low, attended, mixer_exit_coefficients, wo_got, d_middle, q_proj, wqkv, units(own, EARLY), units(give, EARLY - MATED),
+        (gains, mlp_gain_grad),
+        (query, hidden[0], brow, low, attended, mixer_exit_coefficients, wo_got, d_middle, q_proj, wqkv, units(own, EARLY), units(give, EARLY - MATED),
          parts, out_own, keys, values, k_proj, cosine, sine, rows),
     )
     (grad_hidden, out_hidden, attn, wq, wk, wv, q_gain, k_gain, wo, mlp, wg, wu, wd) = result_call(

time: 273 us -> 269 us (0.985)
  no operation moved by 1% of the time
where the time goes in v1:
time: 269 us
  Pallas kernels  268 us (100%)
    pallas_call x1, Pallas kernels, backward_call(): pl.pallas_call(backward_kernel, name='backward', out_shape=outs, in_specs...  146 us
    pallas_call x1, Pallas kernels, forward_call(): pl.pallas_call(forward_kernel, name='forward', out_shape=outs, in_specs=[...  59.2 us
    pallas_call x1, Pallas kernels, mlp_call(): pl.pallas_call(mlp_kernel, name='mlp', out_shape=outs, in_specs=[VMEM_SPE...  56.3 us
    pallas_call x1, Pallas kernels, result_call(): pl.pallas_call(result_kernel, name='result', out_shape=outs, in_specs=[AN...  6.6 us

profile of v1, /device:TPU:0, one launch (start us, length us, event | category | flops | bytes accessed | tf_op | source)
XLA Modules:
  0.0 268.9 jit_solution(6798269268681078142)
XLA Ops:
  0.6 59.2 %forward.1 = (f32[8,1024]{1,0:T(8,128)}, bf16[3,1024,1024]{2,1,0:T(8,128)(2,1)}, f32[1024,512]{1,0:T(8,128)}, f32[3,1024,256]{2,1,0:T(8,128)}, bf16[4,1024,256]{...) custom-call(bf16[256,1024]{1,0:T(8,128)(2,1)} %bitcast.12, ...), custom_call_target="tpu_custom_call" | custom-call | tf_op jit(solution)/shard_map/forward/pallas_call | solution.py:556
  59.8 56.3 %mlp.1 = (f32[256,1024]{1,0:T(8,128)}, f32[8,1024]{1,0:T(8,128)}, bf16[256,1024]{1,0:T(8,128)(2,1)}, bf16[9,256,512]{2,1,0:T(8,128)(2,1)}, bf16[7,256,512]{2,1,0...) custom-call(bf16[1024,512]{1,0:T(8,128)(2,1)} %get-tuple-element.54.low, bf16[256,1024]{1,0:T(8,128)(2,1)} %bitcast.13, ...), custom_call_target="tpu_custom_call" | custom-call | tf_op jit(solution)/shard_map/mlp/pallas_call | solution.py:841
  116.1 146.0 %backward.1 = (bf16[256,1024]{1,0:T(8,128)(2,1)}, f32[256,1024]{1,0:T(8,128)}, f32[8,1024]{1,0:T(8,128)}, bf16[30,128,512]{2,1,0:T(8,128)(2,1)}) custom-call(f32[8,1024]{1,0:T(8,128)} %get-tuple-element.53.gains, f32[8,1024]{1,0:T(8,128)} %get-tuple-element.59.mlp_gain_grad, bf16[4,1024,256]{2,1,0:T(8,128)(2,1)} %get-tuple-element.60.query_in, ...), custom_call_target="tpu_custom_call" | custom-call | tf_op jit(solution)/shard_map/backward/pallas_call | solution.py:1428
  262.1 6.6 %result.1 = (f32[256,1024]{1,0:T(8,128)}, bf16[256,1024]{1,0:T(8,128)(2,1)}, f32[1,512]{1,0:T(1,128)}, f32[512,512]{1,0:T(8,128)}, f32[512,256]{1,0:T(8,128)}, /...) custom-call(bf16[15,256,512]{2,1,0:T(8,128)(2,1)} %bitcast.15, ...), custom_call_target="tpu_custom_call" | custom-call | tf_op jit(solution)/shard_map/result/pallas_call | solution.py:1551

commit v2 on v1

--- a/solution.py
+++ b/solution.py
@@ -940,7 +940,7 @@
 
     def slot(self, k):
         for u in (2 * k, 2 * k + 1):
-            self.first(u)
+            self.run(k < LATE // 2, lambda: self.first(u))
             self.run(k >= 2, lambda: self.second(u - 4))
             self.run(k >= 4, lambda: self.third(u - 8))
 
@@ -1023,7 +1023,8 @@
             copy.wait()
 
     brow_load = locals_.start(brow_in, rowbuf.at[piece(t), :])
-    loads = [locals_.start(own_in, own.at[0:EARLY])]
+    loads = [locals_.start(own_in.at[0:MATED], own.at[0:MATED])]
+    own_load = locals_.start(own_in.at[MATED:EARLY], own.at[MATED:EARLY])
     wo_loads = []
     for j in range(2):
         at = slice(j * 256, j * 256 + 256)
@@ -1078,7 +1079,9 @@
     for copy in loads:
         locals_.wait(copy)
     pump.slot(0)
-    send_early(MATED + 4, 2)
+    pump.slot(1)
+    send_early(MATED + 4, 4)
+    locals_.wait(own_load)
     gkv[...] = jnp.zeros(gkv.shape, f32)
     gsum[...] = jnp.zeros(gsum.shape, f32)
     gsum[1:2, :] = mlp_gain_grad[0:1, :]
@@ -1110,8 +1113,6 @@
         locals_.wait(copy)
     out_far.wait_recv()
     out_buf[0] = out_buf[0] + out_buf[1]
-    pump.slot(1)
-    send_early(MATED + 6, 2)
     b_over.wait_recv()
     b_on.start()
     out_over.start()
@@ -1225,9 +1226,12 @@
         def _():
             tile(2, n // 3, m // 2, (m + 1) // 2, None)
 
+        @pl.when((n & 1) == 1)
+        def _():
+            pump.slot(3 + n // 2)
+
         @pl.when(m == 2)
         def _():
-            pump.slot(3 + n // 3)
             for e in range(2):
                 u = MATED + 10 + 2 * (n // 3) + e
                 pump.to_mate(u, give.at[u - MATED]).start()
@@ -1246,7 +1250,6 @@
     out_far.wait_send()
     out_over.wait_send()
     out_near.wait_send()
-    pump.slot(5)
 
     @pl.when(c >= 1)
     def _():
@@ -1261,9 +1264,9 @@
         def _():
             tile(1, n // 4, m // 2, m & 1, None)
 
-        @pl.when(m == 3)
+        @pl.when((n & 1) == 1)
         def _():
-            pump.slot(6 + n // 4)
+            pump.slot(6 + n // 2)
 
     @pl.when(c >= 2)
     def _():
@@ -1280,7 +1283,7 @@
     def _():
         scatter(scatters[1], 1, kv_part)
 
-    pump.slot(8)
+    pump.slot(10)
     fetched(0)
     clear()
 
@@ -1291,7 +1294,7 @@
 
         @pl.when(n == 3)
         def _():
-            pump.slot(9)
+            pump.slot(11)
 
     finish_kv(0)
 
@@ -1312,7 +1315,7 @@
         for e in range(2):
             late_give[8 + 2 * n + e] = got[e * 128 : e * 128 + 128]
             pump.to_mate(LATE + 4 + 2 * n + e, late_give.at[8 + 2 * n + e]).start()
-    pump.slot(10)
+    pump.slot(12)
 
     @pl.when((c >= 1) & (c < nctx - 1))
     def _():
@@ -1335,9 +1338,6 @@
             at = slice(e * 128, e * 128 + 128)
             own[LATE + 2 * n + e] = rows_of[at]
             own[LATE + 4 + 2 * n + e] = got[at]
-    for u in range(LATE - 4, LATE):
-        pump.second(u)
-        pump.third(u - 4)
     pump.third(LATE - 4)
     pump.third(LATE - 3)
     pl.loop(0, LATE - 8)(pump.fourth)
@@ -1464,7 +1464,7 @@
             pltpu.SemaphoreType.DMA((4 * UNITS,)),
             pltpu.SemaphoreType.DMA((4 * UNITS,)),
             pltpu.SemaphoreType.DMA((UNITS,)),
-            pltpu.SemaphoreType.DMA((21,)),
+            pltpu.SemaphoreType.DMA((22,)),
             pltpu.SemaphoreType.DMA((18,)),
         ],
         compiler_params=pltpu.CompilerParams(

time: 269 us -> 267 us (level)
  no operation moved by 1% of the time
where the time goes in v2:
time: 267 us
  Pallas kernels  266 us (100%)
    pallas_call x1, Pallas kernels, backward_call(): pl.pallas_call(backward_kernel, name='backward', out_shape=outs, in_specs...  144 us
    pallas_call x1, Pallas kernels, forward_call(): pl.pallas_call(forward_kernel, name='forward', out_shape=outs, in_specs=[...  59.2 us
    pallas_call x1, Pallas kernels, mlp_call(): pl.pallas_call(mlp_kernel, name='mlp', out_shape=outs, in_specs=[VMEM_SPE...  56.3 us
    pallas_call x1, Pallas kernels, result_call(): pl.pallas_call(result_kernel, name='result', out_shape=outs, in_specs=[AN...  6.6 us

profile of v2, /device:TPU:0, one launch (start us, length us, event | category | flops | bytes accessed | tf_op | source)
XLA Modules:
  0.0 266.5 jit_solution(10103455974155672580)
XLA Ops:
  0.6 59.2 %forward.1 = (f32[8,1024]{1,0:T(8,128)}, bf16[3,1024,1024]{2,1,0:T(8,128)(2,1)}, f32[1024,512]{1,0:T(8,128)}, f32[3,1024,256]{2,1,0:T(8,128)}, bf16[4,1024,256]{...) custom-call(bf16[256,1024]{1,0:T(8,128)(2,1)} %bitcast.12, ...), custom_call_target="tpu_custom_call" | custom-call | tf_op jit(solution)/shard_map/forward/pallas_call | solution.py:556
  59.8 56.3 %mlp.1 = (f32[256,1024]{1,0:T(8,128)}, f32[8,1024]{1,0:T(8,128)}, bf16[256,1024]{1,0:T(8,128)(2,1)}, bf16[9,256,512]{2,1,0:T(8,128)(2,1)}, bf16[7,256,512]{2,1,0...) custom-call(bf16[1024,512]{1,0:T(8,128)(2,1)} %get-tuple-element.54.low, bf16[256,1024]{1,0:T(8,128)(2,1)} %bitcast.13, ...), custom_call_target="tpu_custom_call" | custom-call | tf_op jit(solution)/shard_map/mlp/pallas_call | solution.py:841
  116.1 143.6 %backward.1 = (bf16[256,1024]{1,0:T(8,128)(2,1)}, f32[256,1024]{1,0:T(8,128)}, f32[8,1024]{1,0:T(8,128)}, bf16[30,128,512]{2,1,0:T(8,128)(2,1)}) custom-call(f32[8,1024]{1,0:T(8,128)} %get-tuple-element.53.gains, f32[8,1024]{1,0:T(8,128)} %get-tuple-element.59.mlp_gain_grad, bf16[4,1024,256]{2,1,0:T(8,128)(2,1)} %get-tuple-element.60.query_in, ...), custom_call_target="tpu_custom_call" | custom-call | tf_op jit(solution)/shard_map/backward/pallas_call | solution.py:1428
  259.7 6.6 %result.1 = (f32[256,1024]{1,0:T(8,128)}, bf16[256,1024]{1,0:T(8,128)(2,1)}, f32[1,512]{1,0:T(1,128)}, f32[512,512]{1,0:T(8,128)}, f32[512,256]{1,0:T(8,128)}, /...) custom-call(bf16[15,256,512]{2,1,0:T(8,128)(2,1)} %bitcast.15, ...), custom_call_target="tpu_custom_call" | custom-call | tf_op jit(solution)/shard_map/result/pallas_call | solution.py:1551

commit v3 on v2

--- a/solution.py
+++ b/solution.py
@@ -676,17 +676,10 @@
     def branch_part(owner):
         return flat_dot(low[piece(owner), :], wo[...])
 
-    @pl.loop(0, 4)
-    def _(n):
-        value = branch_part(t ^ (3 - n))
-        pl.when(n == 0)(lambda: branch.put_far(value))
-        pl.when(n == 1)(lambda: branch.put_over(value))
-        pl.when(n == 2)(lambda: branch.put_near(value))
-
-        @pl.when(n == 3)
-        def _():
-            middle[...] = hidden[...].astype(f32) + value
-
+    branch.put_far(branch_part(t ^ 3))
+    branch.put_over(branch_part(t ^ 2))
+    branch.put_near(branch_part(t ^ 1))
+    middle[...] = hidden[...].astype(f32) + branch_part(t)
     wd_copy.wait_recv()
     wd_on.start()
     middle[...] = branch.total(middle[...])

time: 267 us -> 267 us (level)
  no operation moved by 1% of the time
where the time goes in v3:
time: 267 us
  Pallas kernels  266 us (100%)
    pallas_call x1, Pallas kernels, backward_call(): pl.pallas_call(backward_kernel, name='backward', out_shape=outs, in_specs...  143 us
    pallas_call x1, Pallas kernels, forward_call(): pl.pallas_call(forward_kernel, name='forward', out_shape=outs, in_specs=[...  59.2 us
    pallas_call x1, Pallas kernels, mlp_call(): pl.pallas_call(mlp_kernel, name='mlp', out_shape=outs, in_specs=[VMEM_SPE...  56.6 us
    pallas_call x1, Pallas kernels, result_call(): pl.pallas_call(result_kernel, name='result', out_shape=outs, in_specs=[AN...  6.6 us

profile of v3, /device:TPU:0, one launch (start us, length us, event | category | flops | bytes accessed | tf_op | source)
XLA Modules:
  0.0 266.5 jit_solution(3296662194718005380)
XLA Ops:
  0.6 59.2 %forward.1 = (f32[8,1024]{1,0:T(8,128)}, bf16[3,1024,1024]{2,1,0:T(8,128)(2,1)}, f32[1024,512]{1,0:T(8,128)}, f32[3,1024,256]{2,1,0:T(8,128)}, bf16[4,1024,256]{...) custom-call(bf16[256,1024]{1,0:T(8,128)(2,1)} %bitcast.12, ...), custom_call_target="tpu_custom_call" | custom-call | tf_op jit(solution)/shard_map/forward/pallas_call | solution.py:556
  59.8 56.6 %mlp.1 = (f32[256,1024]{1,0:T(8,128)}, f32[8,1024]{1,0:T(8,128)}, bf16[256,1024]{1,0:T(8,128)(2,1)}, bf16[9,256,512]{2,1,0:T(8,128)(2,1)}, bf16[7,256,512]{2,1,0...) custom-call(bf16[1024,512]{1,0:T(8,128)(2,1)} %get-tuple-element.54.low, bf16[256,1024]{1,0:T(8,128)(2,1)} %bitcast.13, ...), custom_call_target="tpu_custom_call" | custom-call | tf_op jit(solution)/shard_map/mlp/pallas_call | solution.py:834
  116.4 143.3 %backward.1 = (bf16[256,1024]{1,0:T(8,128)(2,1)}, f32[256,1024]{1,0:T(8,128)}, f32[8,1024]{1,0:T(8,128)}, bf16[30,128,512]{2,1,0:T(8,128)(2,1)}) custom-call(f32[8,1024]{1,0:T(8,128)} %get-tuple-element.53.gains, f32[8,1024]{1,0:T(8,128)} %get-tuple-element.59.mlp_gain_grad, bf16[4,1024,256]{2,1,0:T(8,128)(2,1)} %get-tuple-element.60.query_in, ...), custom_call_target="tpu_custom_call" | custom-call | tf_op jit(solution)/shard_map/backward/pallas_call | solution.py:1421
  259.7 6.6 %result.1 = (f32[256,1024]{1,0:T(8,128)}, bf16[256,1024]{1,0:T(8,128)(2,1)}, f32[1,512]{1,0:T(1,128)}, f32[512,512]{1,0:T(8,128)}, f32[512,256]{1,0:T(8,128)}, /...) custom-call(bf16[15,256,512]{2,1,0:T(8,128)(2,1)} %bitcast.15, ...), custom_call_target="tpu_custom_call" | custom-call | tf_op jit(solution)/shard_map/result/pallas_call | solution.py:1544
